TPU v7x, 32 devices: a whole 2x2x4 slice. The times are simulated.
32 devices in a mesh: samp: 8 (over z, core), chan: 4 (over y, x).
Axes of the slice: x: 2, y: 2, z: 4, core: 2. Of those that a mesh axis runs over, the one named last changes fastest.
Arguments:
- out_cot: bfloat16 [8, 256, 4096], P('samp', 'chan'), may hold values from -6 to 6
- mix_weight: bfloat16 [256, 256], replicated, may hold values from -0.375 to 0.375
- corr_kernels: float32 [2, 12, 256, 64], P(None, None, 'chan'), may hold values from -0.75 to 0.75
- momentum: int32 [8], P('samp'), may hold values from 0 to 11
- spin_up: int32 [8, 4096], P('samp', 'chan'), may hold values 0 or 1
- layer_input: bfloat16 [8, 256, 4096], P('samp', None, 'chan'), may hold values from -6 to 6
- pre_one: bfloat16 [8, 256, 4096], P('samp', None, 'chan'), may hold values from -6 to 6
- pre_two: bfloat16 [8, 256, 4096], P('samp', None, 'chan'), may hold values from -6 to 6
- conv_weight: bfloat16 [3, 9, 256, 256], replicated, may hold values from -0.125 to 0.125
- dilation: int32 [3, 256], replicated, may hold values from 1 to 4, as said below
Outputs:
- input_grad: bfloat16 [8, 256, 4096], P('samp', None, 'chan')
- weight_grad: float32 [3, 9, 256, 256], P(None, None, 'chan')
Inputs may be any that keep to these rules, and one draw needn't show every extreme that they name: Some channel of every convolution has dilation 4.
All inputs are finite; a program needn't handle non-finite values. No bound on the sum of `spin_up` on one device may be relied on, other than what follows from the above.
Results may differ from a plain program's by a relative error of at most 0.02.
Values may be sent and summed in bfloat16 or wider, within the bound.
A program may use at most 64 MiB of HBM per device.

v0:
```python
import math

import jax
import jax.numpy as jnp
from jax import lax
from jax.sharding import PartitionSpec as P

SIDE = 64
LAYERS = 3
MAXDIL = 4


def with_halo(shard, sides, width):
    for axis, dim in sides:
        size, length = (lax.axis_size(axis), shard.shape[dim])
        up = [(i, (i + 1) % size) for i in range(size)]
        down = [(j, i) for i, j in up]
        last = lax.slice_in_dim(shard, length - width, length, axis=dim)
        leading = lax.slice_in_dim(shard, 0, width, axis=dim)
        before = lax.ppermute(last, axis, up)
        after = lax.ppermute(leading, axis, down)
        shard = jnp.concatenate([before, shard, after], axis=dim)
    return shard


def column_shift(values, step_size, lattice_side, column):
    if step_size == 0:
        return values
    inside = (column - step_size >= 0) & (column - step_size < lattice_side)
    wrapped = step_size - lattice_side if step_size > 0 else step_size + lattice_side
    return jnp.where(inside, jnp.roll(values, step_size, axis=2), jnp.roll(values, wrapped, axis=2))


def on_device(
    out_cot,
    mix_weight,
    corr_kernels,
    momentum,
    spin_up,
    layer_input,
    pre_one,
    pre_two,
    conv_weight,
    dilation,
):
    highest = lax.Precision.HIGHEST
    sample_count = out_cot.shape[0]
    chan_block = out_cot.shape[1]
    site_count = out_cot.shape[2]
    sectors = corr_kernels.shape[1]
    lattice_side = corr_kernels.shape[3]
    slab_cells = layer_input.shape[2]
    own_start = lax.axis_index("chan") * chan_block
    own_rows = lax.dynamic_slice_in_dim(mix_weight, own_start, chan_block, 0)
    input_cot = lax.psum_scatter(
        jnp.einsum("oc,son->csn", own_rows, out_cot, preferred_element_type=jnp.float32),
        "chan",
        scatter_dimension=0,
        tiled=True,
    )
    onehot = (momentum[:, None] == jnp.arange(sectors, dtype=jnp.int32)[None, :]).astype(
        jnp.float32
    )
    picked = jnp.einsum("sk,akci->acsi", onehot, corr_kernels, precision=highest)
    positions = jnp.arange(lattice_side, dtype=jnp.int32)
    circ_table = (
        (positions[None, None, :] - positions[None, :, None]) % lattice_side
        == positions[:, None, None]
    ).astype(jnp.float32)
    circulant = jnp.einsum("acsi,ixy->acsxy", picked, circ_table, precision=highest)
    grid_values = input_cot.reshape(chan_block, sample_count, lattice_side, lattice_side)
    halfway = jnp.einsum("csxX,csxy->csXy", circulant[0], grid_values, precision=highest)
    corr_grad = jnp.einsum("csXy,csyY->scXY", halfway, circulant[1], precision=highest)
    corr_grad = corr_grad.reshape(sample_count, chan_block, site_count).astype(jnp.bfloat16)
    regrouped = lax.all_to_all(corr_grad, "chan", split_axis=2, concat_axis=1, tiled=True)
    spin_gate = jnp.where(spin_up == 1, 1.5, 0.5).astype(jnp.float32)[:, None, :]
    grad_now = (regrouped.astype(jnp.float32) * spin_gate).astype(jnp.bfloat16)
    halo_cells = MAXDIL * SIDE
    column = jnp.arange(slab_cells, dtype=jnp.int32) % lattice_side
    norm_factor = 1.0 / math.sqrt(sample_count * lax.axis_size("samp") * site_count)
    layer_grads = [None] * LAYERS
    input_grad = None
    for conv_level in range(LAYERS - 1, -1, -1):
        slope_base = None
        if conv_level == 0:
            layer_values = layer_input
        else:
            saved_pre = pre_one if conv_level == 1 else pre_two
            slope_base = jnp.tanh(saved_pre.astype(jnp.float32))
            layer_values = slope_base.astype(jnp.bfloat16)
        padded = with_halo(grad_now, (("chan", 2),), halo_cells)
        back_sum = jnp.zeros(grad_now.shape, jnp.float32)
        tap_grads = []
        for row_step in (-1, 0, 1):
            for col_step in (-1, 0, 1):
                tap_index = (row_step + 1) * 3 + col_step + 1
                if row_step == 0 and col_step == 0:
                    combined = grad_now
                else:
                    combined = None
                    for dilate in range(1, MAXDIL + 1):
                        slice_begin = halo_cells - row_step * dilate * lattice_side
                        shifted = column_shift(
                            padded[:, :, slice_begin : slice_begin + slab_cells],
                            col_step * dilate,
                            lattice_side,
                            column,
                        )
                        if combined is None:
                            combined = shifted
                        else:
                            chosen_mask = (dilation[conv_level] == dilate)[None, :, None]
                            combined = jnp.where(chosen_mask, shifted, combined)
                back_sum = back_sum + jnp.einsum(
                    "oc,son->scn",
                    conv_weight[conv_level, tap_index],
                    combined,
                    preferred_element_type=jnp.float32,
                )
                tap_grads.append(
                    jnp.einsum(
                        "son,scn->oc", combined, layer_values, preferred_element_type=jnp.float32
                    )
                    * norm_factor
                )
        local_grad = jnp.stack(tap_grads)
        reduced = lax.psum_scatter(
            local_grad.astype(jnp.bfloat16), "chan", scatter_dimension=1, tiled=True
        )
        layer_grads[conv_level] = lax.psum(reduced, "samp").astype(jnp.float32)
        if conv_level > 0:
            grad_now = (back_sum * (1.0 - slope_base * slope_base)).astype(jnp.bfloat16)
        else:
            input_grad = back_sum.astype(jnp.bfloat16)
    weight_grad = jnp.stack(layer_grads)
    return (input_grad, weight_grad)


def solution(mesh):
    in_specs = (
        P("samp", "chan", None),
        P(),
        P(None, None, "chan", None),
        P("samp"),
        P("samp", "chan"),
        P("samp", None, "chan"),
        P("samp", None, "chan"),
        P("samp", None, "chan"),
        P(),
        P(),
    )
    out_specs = (P("samp", None, "chan"), P(None, None, "chan", None))
    return jax.shard_map(
        on_device, mesh=mesh, in_specs=in_specs, out_specs=out_specs, check_vma=False
    )
```

profile of v0, /device:TPU:0, one launch (start us, length us, event | category | flops | bytes accessed | tf_op | source)
XLA Modules:
  0.0 344.3 jit_solution(6769106226334867354)
XLA Ops:
  7.2 3.8 %convolution_bitcast_fusion = f32[256,1,4096]{2,0,1:T(8,128)} fusion(bf16[1,64,4096]{2,1,0:T(8,128)(2,1)} %param.10, bf16[256,256]{1,0:T(8,128)(2,1)} %param.11, s32[]{:T(128)S(6)} %select_n.3285), kind=kOutput, calls=%fused_computation | convolution fusion | flops 134217728 | bytes 4751364 | tf_op jit(solution)/shard_map/oc,son->csn/dot_general | solution.py:56
  12.7 1.8 fusion.5
  14.5 2.3 slice_bitcast_fusion
  16.8 49.8 %reduce-scatter.5.cloned.1.call-done = f32[64,1,4096]{2,0,1:T(8,128)} async-done(((f32[256,1,4096]{2,0,1:T(8,128)}), f32[64,1,4096]{2,0,1:T(8,128)}) %reduce-scatter.5.cloned.1.call-update) | async-done | bytes 1048592 | tf_op jit(solution)/shard_map/reduce_scatter | solution.py:55
  66.7 2.2 reshape.16731
  68.8 6.2 %fusion.2 = f32[64,64,64]{2,1,0:T(8,128)S(1)} fusion(f32[64,64,64]{2,1,0:T(8,128)S(1)} %reshape.16731, f32[64,64,64]{2,0,1:T(8,128)} %get-tuple-element.25), kind=kOutput, calls=%fused_computation.119 | convolution fusion | flops 201326592 | bytes 3145728 | tf_op jit(solution)/shard_map/csxX,csxy->csXy/dot_general | solution.py:72
  75.0 3.3 fusion.7
  79.2 2.8 copy.42
  82.5 23.6 %reduce.18 = bf16[4096,64]{1,0:T(8,128)(2,1)} reduce(bf16[4096,1,64]{2,1,0:T(2,128)(2,1)S(1)} %bitcast.976, bf16[]{:T(256)} %broadcast.4323), dimensions={1}, to_apply=%bitcast.918.reduce_sub_computation | reduce | bytes 1048578
  106.1 2.7 reshape.16776
  108.7 3.5 %all-to-all-start = ((bf16[4,2,32768]{2,1,0:T(2,128)(2,1)}), bf16[4,2,32768]{2,1,0:T(2,128)(2,1)S(1)}, u32[]{:S(2)}, u32[]{:S(2)}) async-start(bf16[4,2,32768]{2,1,0:T(2,128)(2,1)} %reshape.16776), calls=%async_computation.1 | async-start | bytes 1048576 | tf_op jit(solution)/shard_map/all_to_all | solution.py:75
  114.4 6.1 %all-to-all-done = bf16[4,2,32768]{2,1,0:T(2,128)(2,1)S(1)} async-done(((bf16[4,2,32768]{2,1,0:T(2,128)(2,1)}), bf16[4,2,32768]{2,1,0:T(2,128)(2,1)S(1)}, u32[]{:S(2)}, u32[]{:S(2)}) %all-to-all-start) | async-done | bytes 524320 | tf_op jit(solution)/shard_map/all_to_all | solution.py:75
  121.3 2.3 copy.43
  126.2 1.5 collective-permute-start.1
  127.7 1.9 collective-permute-start
  129.6 4.8 %collective-permute-done = bf16[1,256,256]{1,2,0:T(8,128)(2,1)S(1)} collective-permute-done((bf16[1,256,256]{1,2,0:T(8,128)(2,1)S(1)}, bf16[1,256,256]{1,2,0:T(8,128)(2,1)S(1)}, u32[]{:S(2)}, u32[]{:S(2)}) %collective-permute-start) | collective-permute-done | bytes 131104 | tf_op jit(solution)/shard_map/ppermute | solution.py:21
  137.4 3.0 fusion.252
  142.1 1.2 convolution_add_fusion.23
  143.4 3.0 fusion.256
  146.4 1.2 convolution_add_fusion.22
  147.6 3.0 fusion.260
  150.6 1.2 convolution_add_fusion.21
  151.8 1.3 convolution_add_fusion.20
  153.1 3.0 fusion.264
  156.1 1.2 convolution_add_fusion.19
  157.4 3.0 fusion.268
  160.4 1.2 convolution_add_fusion.18
  161.6 1.2 convolution_add_fusion.17
  162.9 3.0 fusion.272
  165.9 1.2 fusion.14
  168.8 2.0 collective-permute-start.2
  177.7 3.0 fusion.276
  182.4 1.2 convolution_add_fusion.15
  183.7 3.0 fusion.280
  186.7 1.2 convolution_add_fusion.14
  187.9 3.0 fusion.284
  190.9 1.2 convolution_add_fusion.13
  192.2 1.2 convolution_add_fusion.12
  193.4 3.0 fusion.288
  196.4 1.2 convolution_add_fusion.11
  197.6 3.0 fusion.292
  200.7 1.2 convolution_add_fusion.10
  201.9 1.2 convolution_add_fusion.9
  203.1 3.0 fusion.296
  206.2 1.2 fusion.15
  208.5 2.0 collective-permute-start.4
  218.1 3.0 fusion.300
  223.8 3.0 fusion.304
  227.8 3.0 fusion.308
  232.9 3.0 fusion.312
  236.8 3.0 fusion.316
  241.9 3.0 fusion.320
  245.9 1.2 fusion.435
  247.1 1.2 convolution_add_fusion.7
  248.3 1.2 convolution_add_fusion.6
  249.6 1.3 convolution_add_fusion.5
  250.8 1.3 convolution_add_fusion.4
  252.1 1.2 convolution_add_fusion.3
  253.4 1.3 convolution_add_fusion.2
  254.7 20.1 %reduce-scatter.7.cloned.1.call-done = bf16[9,64,256]{2,1,0:T(8,128)(2,1)} async-done(((bf16[9,256,256]{2,1,0:T(8,128)(2,1)}), bf16[9,64,256]{2,1,0:T(8,128)(2,1)}) %reduce-scatter.7.cloned.1.call-update) | async-done | bytes 294928 | tf_op jit(solution)/shard_map/reduce_scatter | solution.py:127
  274.9 1.2 convolution_add_fusion.1
  276.1 1.3 fusion.17
  278.4 56.7 %all-reduce.3.cloned.1.call-done = (bf16[1,9,64,256]{3,2,1,0:T(8,128)(2,1)}, bf16[1,9,64,256]{3,2,1,0:T(8,128)(2,1)}, bf16[1,9,64,256]{3,2,1,0:T(8,128)(2,1)}) async-done(((bf16[1,9,64,256]{3,2,1,0:T(8,128)(2,1)}, bf16[1,9,64,256]{3,2,1,0:T(8,128)(2,1)}, bf16[1,9,64,256]{3,2,1,0:T(8,128)(2,1)}), (bf16[1,9,64,256]{3,2,1,0:T(8,128)(2,1)}, bf16[1,9,64,256]{3,2,1,0:T(8,128)(2,1)}, ...) | async-done | bytes 884752 | tf_op jit(solution)/shard_map/psum | solution.py:130
  335.0 2.5 maximum_convert_fusion
  (210 shorter events, 41.9 us)
Async XLA Ops:
  7.2 4.7 %copy-start = (f32[2,12,64,64]{3,2,1,0:T(8,128)S(1)}, f32[2,12,64,64]{3,2,1,0:T(8,128)}, u32[]{:S(2)}) copy-start(f32[2,12,64,64]{3,2,1,0:T(8,128)} %param.12) | copy-start | bytes 1179652
  7.2 59.5 %reduce-scatter.5.cloned.1.call-start = ((), (), s32[]{:S(2)}) async-start(), calls=%async_computation.5 | async-start | bytes 5242880 | tf_op jit(solution)/shard_map/reduce_scatter | solution.py:55
  68.8 6.2 %copy-start.2 = (f32[64,64,64]{2,0,1:T(8,128)S(1)}, f32[64,64,64]{2,0,1:T(8,128)}, u32[]{:S(2)}) copy-start(f32[64,64,64]{2,0,1:T(8,128)} %get-tuple-element.24) | copy-start | bytes 3145732
  106.1 6.2 %copy-start.15 = (bf16[1,256,1024]{2,1,0:T(8,128)(2,1)S(1)}, bf16[1,256,1024]{2,1,0:T(8,128)(2,1)}, u32[]{:S(2)}) copy-start(bf16[1,256,1024]{2,1,0:T(8,128)(2,1)} %param.16) | copy-start | bytes 1572868
  106.1 7.2 %copy-start.16 = (bf16[1,256,1024]{2,1,0:T(8,128)(2,1)S(1)}, bf16[1,256,1024]{2,1,0:T(8,128)(2,1)}, u32[]{:S(2)}) copy-start(bf16[1,256,1024]{2,1,0:T(8,128)(2,1)} %param.17) | copy-start | bytes 1572868
  106.1 8.2 %copy-start.18 = (s32[3,256]{1,0:T(4,128)S(1)}, s32[3,256]{1,0:T(4,128)}, u32[]{:S(2)}) copy-start(s32[3,256]{1,0:T(4,128)} %param.19) | copy-start | bytes 9220
  106.1 8.3 %copy-start.17 = (s32[1,1024]{1,0:T(1,128)S(1)}, s32[1,1024]{1,0:T(1,128)}, u32[]{:S(2)}) copy-start(s32[1,1024]{1,0:T(1,128)} %param.14) | copy-start | bytes 12292
  108.7 11.7 %all-to-all-start = ((bf16[4,2,32768]{2,1,0:T(2,128)(2,1)}), bf16[4,2,32768]{2,1,0:T(2,128)(2,1)S(1)}, u32[]{:S(2)}, u32[]{:S(2)}) async-start(bf16[4,2,32768]{2,1,0:T(2,128)(2,1)} %reshape.16776), calls=%async_computation.1 | async-start | bytes 1048576 | tf_op jit(solution)/shard_map/all_to_all | solution.py:75
  112.2 142.5 %reduce-scatter.11.cloned.1.call-start = ((), (), s32[]{:S(2)}) async-start(), calls=%async_computation.8 | async-start | bytes 1474560 | tf_op jit(solution)/shard_map/reduce_scatter | solution.py:127
  126.2 8.3 %collective-permute-start.1 = (bf16[1,256,256]{1,2,0:T(8,128)(2,1)S(1)}, bf16[1,256,256]{1,2,0:T(8,128)(2,1)S(1)}, u32[]{:S(2)}, u32[]{:S(2)}) collective-permute-start(bf16[1,256,256]{1,2,0:T(8,128)(2,1)S(1)} %get-tuple-element.324), channel_id=1, source_target_pairs={{0,1},{1,2},{2,3},{3,0},{4,5},{5,6},{6,7},{7,4},{8,9},{9,10},{10,1... | collective-permute-start | bytes 393224 | tf_op jit(solution)/shard_map/ppermute | solution.py:20
  127.7 6.7 %collective-permute-start = (bf16[1,256,256]{1,2,0:T(8,128)(2,1)S(1)}, bf16[1,256,256]{1,2,0:T(8,128)(2,1)S(1)}, u32[]{:S(2)}, u32[]{:S(2)}) collective-permute-start(bf16[1,256,256]{1,2,0:T(8,128)(2,1)S(1)} %get-tuple-element.325), channel_id=1, source_target_pairs={{1,0},{2,1},{3,2},{0,3},{5,4},{6,5},{7,6},{4,7},{9,8},{10,9},{11,1... | collective-permute-start | bytes 393224 | tf_op jit(solution)/shard_map/ppermute | solution.py:21
  162.9 3.0 copy-start.8
  167.7 7.3 %collective-permute-start.3 = (bf16[1,256,256]{1,2,0:T(8,128)(2,1)S(1)}, bf16[1,256,256]{1,2,0:T(8,128)(2,1)S(1)}, u32[]{:S(2)}, u32[]{:S(2)}) collective-permute-start(bf16[1,256,256]{1,2,0:T(8,128)(2,1)S(1)} %get-tuple-element.258), channel_id=1, source_target_pairs={{0,1},{1,2},{2,3},{3,0},{4,5},{5,6},{6,7},{7,4},{8,9},{9,10},{10,1... | collective-permute-start | bytes 393224 | tf_op jit(solution)/shard_map/ppermute | solution.py:20
  168.8 6.1 %collective-permute-start.2 = (bf16[1,256,256]{1,2,0:T(8,128)(2,1)S(1)}, bf16[1,256,256]{1,2,0:T(8,128)(2,1)S(1)}, u32[]{:S(2)}, u32[]{:S(2)}) collective-permute-start(bf16[1,256,256]{1,2,0:T(8,128)(2,1)S(1)} %get-tuple-element.259), channel_id=1, source_target_pairs={{1,0},{2,1},{3,2},{0,3},{5,4},{6,5},{7,6},{4,7},{9,8},{10,9},{11,1... | collective-permute-start | bytes 393224 | tf_op jit(solution)/shard_map/ppermute | solution.py:21
  173.8 1.0 copy-start.13
  174.8 79.9 %reduce-scatter.9.cloned.1.call-start = ((), (), s32[]{:S(2)}) async-start(), calls=%async_computation.7 | async-start | bytes 1474560 | tf_op jit(solution)/shard_map/reduce_scatter | solution.py:127
  203.1 3.0 copy-start.7
  207.6 7.8 %collective-permute-start.5 = (bf16[1,256,256]{1,2,0:T(8,128)(2,1)S(1)}, bf16[1,256,256]{1,2,0:T(8,128)(2,1)S(1)}, u32[]{:S(2)}, u32[]{:S(2)}) collective-permute-start(bf16[1,256,256]{1,2,0:T(8,128)(2,1)S(1)} %get-tuple-element.192), channel_id=1, source_target_pairs={{0,1},{1,2},{2,3},{3,0},{4,5},{5,6},{6,7},{7,4},{8,9},{9,10},{10,1... | collective-permute-start | bytes 393224 | tf_op jit(solution)/shard_map/ppermute | solution.py:20
  208.5 6.8 %collective-permute-start.4 = (bf16[1,256,256]{1,2,0:T(8,128)(2,1)S(1)}, bf16[1,256,256]{1,2,0:T(8,128)(2,1)S(1)}, u32[]{:S(2)}, u32[]{:S(2)}) collective-permute-start(bf16[1,256,256]{1,2,0:T(8,128)(2,1)S(1)} %get-tuple-element.193), channel_id=1, source_target_pairs={{1,0},{2,1},{3,2},{0,3},{5,4},{6,5},{7,6},{4,7},{9,8},{10,9},{11,1... | collective-permute-start | bytes 393224 | tf_op jit(solution)/shard_map/ppermute | solution.py:21
  213.9 1.0 copy-start.14
  215.0 59.8 %reduce-scatter.7.cloned.1.call-start = ((), (), s32[]{:S(2)}) async-start(), calls=%async_computation.6 | async-start | bytes 1474560 | tf_op jit(solution)/shard_map/reduce_scatter | solution.py:127
  218.1 3.0 copy-start.19
  222.7 4.1 %copy-start.11 = (bf16[256,1024]{0,1:T(8,128)(2,1)}, bf16[256,1024]{0,1:T(8,128)(2,1)S(1)}, u32[]{:S(2)}) copy-start(bf16[256,1024]{0,1:T(8,128)(2,1)S(1)} %get-tuple-element.123) | copy-start | bytes 1572868
  222.7 18.2 %copy-start.9 = (bf16[256,1024]{0,1:T(8,128)(2,1)}, bf16[256,1024]{0,1:T(8,128)(2,1)S(1)}, u32[]{:S(2)}) copy-start(bf16[256,1024]{0,1:T(8,128)(2,1)S(1)} %get-tuple-element.122) | copy-start | bytes 1572868
  235.8 4.0 %copy-start.3 = (bf16[256,1024]{0,1:T(8,128)(2,1)}, bf16[256,1024]{0,1:T(8,128)(2,1)S(1)}, u32[]{:S(2)}) copy-start(bf16[256,1024]{0,1:T(8,128)(2,1)S(1)} %fusion.312) | copy-start | bytes 1572868
  239.8 2.0 copy-start.5
  244.8 2.3 copy-start.12
  245.9 89.1 %all-reduce.3.cloned.1.call-start = ((), (), s32[]{:S(2)}) async-start(), calls=%async_computation.9 | async-start | bytes 1769472 | tf_op jit(solution)/shard_map/psum | solution.py:130
  249.6 2.6 copy-start.4
  250.8 2.5 copy-start.6
  253.4 21.5 %copy-start.10 = (bf16[256,1024]{0,1:T(8,128)(2,1)S(1)}, bf16[256,1024]{0,1:T(8,128)(2,1)}, u32[]{:S(2)}) copy-start(bf16[256,1024]{0,1:T(8,128)(2,1)} %copy-done.9) | copy-start | bytes 1572868
  276.1 61.5 %copy-start.1 = (f32[2,12,64,64]{3,2,1,0:T(8,128)S(1)}, f32[2,12,64,64]{3,2,1,0:T(8,128)}, u32[]{:S(2)}) copy-start(f32[2,12,64,64]{3,2,1,0:T(8,128)} %param.12) | copy-start | bytes 1179652
Sparse Core Ops, SparseCore 0:
  11.2 55.3 reduce-scatter.4
  174.9 27.8 reduce-scatter.10
  215.1 28.0 reduce-scatter.8
  246.3 28.5 reduce-scatter.6
  277.4 57.5 all-reduce.2
where the time goes:
time: 348 us; the launch traced here: 344 us
  waiting for transfers between devices  138 us (40%)
  other arithmetic  90.3 us (26%)
  matrix products  64.6 us (19%)
  local copies, waits for them, and re-layouts  22.2 us (6%)
  between operations  16.2 us (5%)
  starting transfers between devices  13.4 us (4%)
    psum x1, waiting for transfers between devices, on_device(): layer_grads[conv_level] = lax.psum(reduced, 'samp').astype(jnp.float32)  56.7 us
    select_n x18, other arithmetic, on_device(): combined = jnp.where(chosen_mask, shifted, combined)  54 us
    reduce_scatter x1, waiting for transfers between devices, on_device(): lax.psum_scatter(jnp.einsum('oc,son->csn', own_rows, out_cot, preferred_e...  49.8 us
    dot_general x27, matrix products, on_device(): jnp.einsum('oc,son->scn', conv_weight[conv_level, tap_index], combined, p...  32.9 us
    unnamed x1, other arithmetic  23.6 us
    reduce_scatter x3, waiting for transfers between devices, on_device(): lax.psum_scatter(local_grad.astype(jnp.bfloat16), 'chan', scatter_dimensi...  20.1 us
    dot_general x27, matrix products, on_device(): jnp.einsum('son,scn->oc', combined, layer_values, preferred_element_type=...  15.7 us
    unnamed x46, local copies, waits for them, and re-layouts  9.22 us
  transfers between devices with their start and end apart: 12, of which 5 were waited for; matrix products, arithmetic and copies ran while one was open for 26% of the time, Pallas kernels for 0%

commit v1 on v0

v1 whole, which is shorter than its diff:
```python
import functools
import math

import jax
import jax.numpy as jnp
from jax import lax
from jax.experimental import pallas as pl
from jax.experimental.pallas import tpu as pltpu
from jax.sharding import PartitionSpec as P

SIDE = 64
LAYERS = 3
MAXDIL = 4
HALO = MAXDIL * SIDE
MESH = pl.DeviceIdType.MESH
VMEM = pl.BlockSpec(memory_space=pltpu.VMEM)
VMEM_LIMIT = 48 * 1024 * 1024


def enter(n):
    me = lax.axis_index("chan")
    barrier = pltpu.get_barrier_semaphore()
    for off in range(1, n):
        pl.semaphore_signal(
            barrier, inc=1, device_id={"chan": lax.rem(me + off, n)}, device_id_type=MESH
        )
    pl.semaphore_wait(barrier, n - 1)
    return me


def gather_kernel(n, x_ref, g_ref, xo_ref, go_ref, x_send, x_recv, g_send, g_recv, own):
    rows = x_ref.shape[0]
    me = enter(n)
    place = pl.ds(pl.multiple_of(me * rows, rows), rows)
    copies = []
    for off in range(1, n):
        peer = {"chan": lax.rem(me + off, n)}
        copies.append(
            pltpu.make_async_remote_copy(
                src_ref=x_ref, dst_ref=xo_ref.at[place],
                send_sem=x_send.at[off - 1], recv_sem=x_recv.at[off - 1],
                device_id=peer, device_id_type=MESH,
            )
        )
        copies.append(
            pltpu.make_async_remote_copy(
                src_ref=g_ref, dst_ref=go_ref.at[me],
                send_sem=g_send.at[off - 1], recv_sem=g_recv.at[off - 1],
                device_id=peer, device_id_type=MESH,
            )
        )
    copies.append(pltpu.make_async_copy(x_ref, xo_ref.at[place], own.at[0]))
    copies.append(pltpu.make_async_copy(g_ref, go_ref.at[me], own.at[1]))
    for copy in copies:
        copy.start()
    for copy in copies:
        copy.wait()


def gather(n, x, gate):
    rows, cells = x.shape
    return pl.pallas_call(
        functools.partial(gather_kernel, n),
        out_shape=(
            jax.ShapeDtypeStruct((n * rows, cells), x.dtype),
            jax.ShapeDtypeStruct((n,) + gate.shape, gate.dtype),
        ),
        in_specs=[VMEM, VMEM],
        out_specs=(VMEM, VMEM),
        scratch_shapes=[pltpu.SemaphoreType.DMA((n - 1,))] * 4 + [pltpu.SemaphoreType.DMA((2,))],
        compiler_params=pltpu.CompilerParams(
            collective_id=0, has_side_effects=True, vmem_limit_bytes=VMEM_LIMIT
        ),
        name="gather_blocks",
    )(x, gate)


def regroup_kernel(n, x_ref, o_ref, send, recv, own):
    rows, cells = x_ref.shape
    slab = cells // n
    me = enter(n)
    place = pl.ds(pl.multiple_of(me * rows, rows), rows)
    pieces = ((-HALO, 0, HALO), (0, HALO, slab), (slab, HALO + slab, HALO))
    copies = []
    for off in range(n):
        to = lax.rem(me + off, n)
        for piece, (shift, at, width) in enumerate(pieces):
            begin = pl.multiple_of(lax.rem(to * slab + shift + cells, cells), 128)
            src = x_ref.at[:, pl.ds(begin, width)]
            dst = o_ref.at[place, pl.ds(at, width)]
            if off == 0:
                copies.append(pltpu.make_async_copy(src, dst, own.at[piece]))
            else:
                copies.append(
                    pltpu.make_async_remote_copy(
                        src_ref=src, dst_ref=dst,
                        send_sem=send.at[off - 1, piece], recv_sem=recv.at[off - 1, piece],
                        device_id={"chan": to}, device_id_type=MESH,
                    )
                )
    for copy in copies[3:] + copies[:3]:
        copy.start()
    for copy in copies:
        copy.wait()


def regroup(n, x):
    rows, cells = x.shape
    return pl.pallas_call(
        functools.partial(regroup_kernel, n),
        out_shape=jax.ShapeDtypeStruct((n * rows, cells // n + 2 * HALO), x.dtype),
        in_specs=[VMEM],
        out_specs=VMEM,
        scratch_shapes=[pltpu.SemaphoreType.DMA((n - 1, 3))] * 2 + [pltpu.SemaphoreType.DMA((3,))],
        compiler_params=pltpu.CompilerParams(
            collective_id=1, has_side_effects=True, vmem_limit_bytes=VMEM_LIMIT
        ),
        name="regroup_rows",
    )(x)


def layer_kernel(level, norm, *refs):
    if level == LAYERS - 1:
        padded, dil, saved, weight, out, grads, col, taps = refs
    else:
        before, inner, after, dil, saved, weight, out, grads, col, taps = refs
    chans = weight.shape[1]
    cells = saved.shape[1]
    rows = cells // SIDE
    if level == LAYERS - 1:
        for start in range(0, cells + 2 * HALO, 256):
            block = padded[:, start : start + 256].astype(jnp.float32)
            col[1, start : start + 256, :] = block.T.astype(jnp.bfloat16)
    else:
        col[1, :HALO, :] = before[...]
        col[1, HALO : HALO + cells, :] = inner[...]
        col[1, HALO + cells :, :] = after[...]
    step = dil[...]

    def shift_columns(r, carry):
        at = pl.ds(pl.multiple_of(r * SIDE, SIDE), SIDE)
        value = col[1, at, :].astype(jnp.float32)
        for sign in (-1, 1):
            chosen = pltpu.roll(value, sign % SIDE, 0)
            for d in range(2, MAXDIL + 1):
                chosen = jnp.where(step == d, pltpu.roll(value, (sign * d) % SIDE, 0), chosen)
            col[sign + 1, at, :] = chosen.astype(jnp.bfloat16)
        return carry

    lax.fori_loop(0, rows + 2 * MAXDIL, shift_columns, 0)

    picks = [(step == d).astype(jnp.float32).astype(jnp.bfloat16) for d in range(1, MAXDIL + 1)]

    def shift_rows(r, carry):
        at = pl.ds(pl.multiple_of(r * SIDE, SIDE), SIDE)
        for i in (-1, 0, 1):
            for j in (-1, 0, 1):
                tap = 3 * (i + 1) + j + 1
                if i == 0:
                    value = col[j + 1, pl.ds(pl.multiple_of((r + MAXDIL) * SIDE, SIDE), SIDE), :]
                else:
                    value = None
                    for d in range(1, MAXDIL + 1):
                        begin = pl.multiple_of((r + MAXDIL - i * d) * SIDE, SIDE)
                        term = col[j + 1, pl.ds(begin, SIDE), :] * picks[d - 1]
                        value = term if value is None else value + term
                taps[at, tap * chans : (tap + 1) * chans] = value
        return carry

    lax.fori_loop(0, rows, shift_rows, 0)

    if level == 0:
        act = saved[...]
    else:
        act = jnp.tanh(saved[...].astype(jnp.float32)).astype(jnp.bfloat16)
    flat_weight = weight[...].reshape(9 * chans, chans)
    for start in range(0, cells, 256):
        back = jnp.dot(
            taps[start : start + 256, :], flat_weight, preferred_element_type=jnp.float32
        )
        if level == 0:
            out[:, start : start + 256] = back.T.astype(jnp.bfloat16)
        else:
            slope = jnp.tanh(saved[:, start : start + 256].astype(jnp.float32))
            slope = 1.0 - slope * slope
            out[start : start + 256, :] = (back * slope.T).astype(jnp.bfloat16)
    for tap in range(9):
        term = jnp.dot(
            act, taps[:, tap * chans : (tap + 1) * chans], preferred_element_type=jnp.float32
        )
        grads[tap] = (term * norm).T.astype(jnp.bfloat16)


def layer(level, norm, parts, dil, saved, weight):
    chans, cells = saved.shape
    out_dims = (chans, cells) if level == 0 else (cells, chans)
    flops = 2 * 2 * 9 * chans * chans * cells
    return pl.pallas_call(
        functools.partial(layer_kernel, level, norm),
        out_shape=(
            jax.ShapeDtypeStruct(out_dims, jnp.bfloat16),
            jax.ShapeDtypeStruct((9, chans, chans), jnp.bfloat16),
        ),
        in_specs=[VMEM] * (len(parts) + 3),
        out_specs=(VMEM, VMEM),
        scratch_shapes=[
            pltpu.VMEM((3, cells + 2 * HALO, chans), jnp.bfloat16),
            pltpu.VMEM((cells, 9 * chans), jnp.bfloat16),
        ],
        compiler_params=pltpu.CompilerParams(vmem_limit_bytes=VMEM_LIMIT),
        cost_estimate=pl.CostEstimate(
            flops=flops, bytes_accessed=8 * 1024 * 1024, transcendentals=chans * cells
        ),
        name="conv_backward",
    )(*parts, dil, saved, weight)


def on_device(
    out_cot,
    mix_weight,
    corr_kernels,
    momentum,
    spin_up,
    layer_input,
    pre_one,
    pre_two,
    conv_weight,
    dilation,
):
    chan_block = out_cot.shape[1]
    site_count = out_cot.shape[2]
    side = corr_kernels.shape[3]
    n = lax.axis_size("chan")
    slab = layer_input.shape[2]
    own_start = lax.axis_index("chan") * chan_block
    gate = jnp.where(spin_up == 1, 1.5, 0.5).astype(jnp.float32)
    gate = jnp.broadcast_to(gate, (8, slab))
    everything, gates = gather(n, out_cot[0], gate)
    gates = gates[:, 0, :].reshape(1, side, side)
    own_columns = lax.dynamic_slice_in_dim(mix_weight, own_start, chan_block, 1)
    input_cot = jnp.einsum(
        "oc,on->cn", own_columns, everything, preferred_element_type=jnp.float32
    )
    picked = lax.dynamic_index_in_dim(corr_kernels, momentum[0], axis=1, keepdims=False)
    positions = jnp.arange(side, dtype=jnp.int32)
    circ_table = (
        (positions[None, :] - positions[:, None]) % side == positions[:, None, None]
    ).astype(jnp.float32)
    circulant = jnp.einsum(
        "aci,ixy->acxy", picked, circ_table, precision=lax.Precision.HIGHEST
    )
    grid_values = input_cot.reshape(chan_block, side, side)
    high = lax.Precision.HIGH
    halfway = jnp.einsum("cxX,cxy->cXy", circulant[0], grid_values, precision=high)
    corr_grad = jnp.einsum("cXy,cyY->cXY", halfway, circulant[1], precision=high)
    corr_grad = corr_grad.astype(jnp.bfloat16).astype(jnp.float32)
    gated = (corr_grad * gates).astype(jnp.bfloat16).reshape(chan_block, site_count)
    padded = regroup(n, gated)
    norm = 1.0 / math.sqrt(out_cot.shape[0] * lax.axis_size("samp") * site_count)
    up = [(i, (i + 1) % n) for i in range(n)]
    down = [(j, i) for i, j in up]
    saved = (layer_input[0], pre_one[0], pre_two[0])
    layer_grads = [None] * LAYERS
    parts = (padded,)
    result = None
    for level in range(LAYERS - 1, -1, -1):
        result, local_grad = layer(
            level, norm, parts, dilation[level][None, :], saved[level], conv_weight[level]
        )
        reduced = lax.psum_scatter(local_grad, "chan", scatter_dimension=1, tiled=True)
        layer_grads[level] = lax.psum(reduced, "samp").astype(jnp.float32)
        if level > 0:
            before = lax.ppermute(result[slab - HALO :], "chan", up)
            after = lax.ppermute(result[:HALO], "chan", down)
            parts = (before, result, after)
    return (result[None], jnp.stack(layer_grads))


def solution(mesh):
    in_specs = (
        P("samp", "chan", None),
        P(),
        P(None, None, "chan", None),
        P("samp"),
        P("samp", "chan"),
        P("samp", None, "chan"),
        P("samp", None, "chan"),
        P("samp", None, "chan"),
        P(),
        P(),
    )
    out_specs = (P("samp", None, "chan"), P(None, None, "chan", None))
    return jax.shard_map(
        on_device, mesh=mesh, in_specs=in_specs, out_specs=out_specs, check_vma=False
    )
```

time: 348 us -> 238 us (0.68)
  other arithmetic: 90.3 us -> 2.51 us
  Pallas kernels: 0 us -> 57.3 us
  matrix products: 64.6 us -> 10.1 us
  waiting for transfers between devices: 138 us -> 129 us
  starting transfers between devices: 13.4 us -> 6.12 us
  local copies, waits for them, and re-layouts: 22.2 us -> 17.7 us
    pallas_call x0 -> x5, Pallas kernels: none -> 57.3 us  [the longest x1 29 us: gather(): pl.pallas_call(functools.partial(gather_kernel, n), out_shape=(jax.ShapeD...]
    dot_general x59 -> x4, matrix products: 64.6 us -> 10.1 us  [the longest x1 4.47 us: on_device(): jnp.einsum('cxX,cxy->cXy', circulant[0], grid_values, precision=high)]
    select_n x20 -> x2, other arithmetic: 54 us -> 0.03 us  [the longest x1 0.02 us: on_device(): (positions[None, :] - positions[:, None]) % side == positions[:, None, None]]
    unnamed x1 -> x0, other arithmetic: 23.6 us -> none
    reduce_scatter x4 -> x3, waiting for transfers between devices: 70 us -> 57.1 us  [on_device(): lax.psum_scatter(local_grad, 'chan', scatter_dimension=1, tiled=True)]
    concatenate x24 -> x0, other arithmetic: 8.24 us -> none  [the longest x12 4.23 us: column_shift(): jnp.roll(values, wrapped, axis=2)]
    ppermute x6 -> x4, waiting for transfers between devices: 4.82 us -> 11.7 us  [the longest x2 7.07 us: on_device(): before = lax.ppermute(result[slab - HALO:], 'chan', up)]
    all_to_all x1 -> x0, waiting for transfers between devices: 6.09 us -> none  [on_device(): lax.all_to_all(corr_grad, 'chan', split_axis=2, concat_axis=1, tiled=True)]
  transfers between devices with their start and end apart: 12 -> 8, of which waited for: 5 -> 7; matrix products, arithmetic and copies ran while one was open for 26% -> 1% of each run, Pallas kernels for 0% -> 5%
where the time goes in v1:
time: 238 us; the launch traced here: 237 us
  waiting for transfers between devices  129 us (54%)
  Pallas kernels  57.3 us (24%)
  local copies, waits for them, and re-layouts  17.7 us (7%)
  between operations  14.7 us (6%)
  matrix products  10.1 us (4%)
  starting transfers between devices  6.12 us (3%)
  other arithmetic  2.51 us (1%)
    psum x1, waiting for transfers between devices, on_device(): layer_grads[level] = lax.psum(reduced, 'samp').astype(jnp.float32)  59.9 us
    reduce_scatter x3, waiting for transfers between devices, on_device(): lax.psum_scatter(local_grad, 'chan', scatter_dimension=1, tiled=True)  57.1 us
    pallas_call x1, Pallas kernels, gather(): pl.pallas_call(functools.partial(gather_kernel, n), out_shape=(jax.ShapeD...  29 us
    pallas_call x3, Pallas kernels, layer(): pl.pallas_call(functools.partial(layer_kernel, level, norm), out_shape=(j...  16.2 us
    pallas_call x1, Pallas kernels, regroup(): pl.pallas_call(functools.partial(regroup_kernel, n), out_shape=jax.ShapeD...  12.2 us
    unnamed x30, local copies, waits for them, and re-layouts  8.21 us
    ppermute x2, waiting for transfers between devices, on_device(): before = lax.ppermute(result[slab - HALO:], 'chan', up)  7.07 us
  transfers between devices with their start and end apart: 8, of which 7 were waited for; matrix products, arithmetic and copies ran while one was open for 1% of the time, Pallas kernels for 5%

profile of v1, /device:TPU:0, one launch (start us, length us, event | category | flops | bytes accessed | tf_op | source)
XLA Modules:
  0.0 237.2 jit_solution(9841905739169564310)
XLA Ops:
  7.2 0.0 copy-start
  7.2 0.0 reduce-scatter.8.cloned.1.call-start
  8.0 0.4 copy-done
  8.3 1.8 fusion.5
  10.1 0.0 copy-start.13
  10.1 0.0 copy-start.3
  10.1 0.0 copy-start.12
  10.2 2.3 slice_bitcast_fusion
  12.4 0.0 copy-done.13
  12.4 0.0 copy-done.3
  12.4 29.0 %gather_blocks.1 = (bf16[256,4096]{1,0:T(8,128)(2,1)S(1)}, f32[4,8,1024]{2,1,0:T(8,128)S(1)}) custom-call(bf16[64,4096]{1,0:T(8,128)(2,1)S(1)} %bitcast.35, f32[8,1024]{1,0:T(8,128)S(1)} %broadcast_in_dim.25.g_ref), custom_call_target="tpu_custom_call" | custom-call | tf_op jit(solution)/shard_map/gather_blocks/pallas_call | solution.py:62
  41.4 0.0 copy-done.12
  41.4 1.6 fusion.14
  43.0 2.0 reshape.34
  45.0 0.1 mul.14
  45.1 0.0 copy-start.11
  45.1 4.5 %fusion = f32[64,64,64]{2,1,0:T(8,128)S(1)} fusion(f32[64,64,64]{2,1,0:T(8,128)S(1)} %reshape.34, f32[64,64,64]{2,0,1:T(8,128)} %get-tuple-element.22), kind=kOutput, calls=%fused_computation.2 | convolution fusion | flops 100663296 | bytes 3145728 | tf_op jit(solution)/shard_map/cxX,cxy->cXy/dot_general | solution.py:254
  49.6 0.0 copy-done.11
  49.6 2.3 multiply_convert_fusion
  51.9 0.8 reshape.35.x_ref
  52.8 12.2 %regroup_rows.1.refs_0_ = bf16[256,1536]{1,0:T(8,128)(2,1)S(1)} custom-call(bf16[64,4096]{1,0:T(8,128)(2,1)S(1)} %reshape.35.x_ref), custom_call_target="tpu_custom_call" | custom-call | tf_op jit(solution)/shard_map/regroup_rows/pallas_call | solution.py:109
  64.9 0.0 copy-start.14
  64.9 0.0 copy-start.8
  64.9 2.3 slice_bitcast_fusion.2
  67.3 0.0 copy-done.14
  67.3 0.0 copy-done.8
  67.3 5.1 %conv_backward.3 = (bf16[1024,256]{1,0:T(8,128)(2,1)S(1)}, bf16[9,256,256]{2,1,0:T(8,128)(2,1)S(1)}) custom-call(bf16[256,1536]{1,0:T(8,128)(2,1)S(1)} %regroup_rows.1.refs_0_, s32[1,256]{1,0:T(1,128)S(1)} %get-tuple-element.31.refs_1_, bf16[256,1024]{1,0:T(8,128)(2,1)S(1)} %bitcast.36, bf16[9,256,256]{2,1,0:T(8,128)(2,1)S(1)} %get-tuple-element.24.refs_3_), custom_call_target="tpu_custom_call" | custom-call | flops 2415919104 | bytes 8388608 | tf_op jit(solution)/shard_map/conv_backward/pallas_call | solution.py:198
  72.4 0.0 copy-start.1
  72.4 1.0 copy-done.1
  73.5 0.0 copy-start.6
  73.5 0.8 copy-done.6
  74.3 0.0 reduce-scatter.8.cloned.1.call-update
  74.3 0.0 reduce-scatter.6.cloned.1.call-start
  74.3 1.0 fusion.24
  75.3 0.6 collective-permute-start
  75.9 2.4 %collective-permute-start.1 = (bf16[256,256]{1,0:T(8,128)(2,1)S(1)}, bf16[256,256]{1,0:T(8,128)(2,1)S(1)}, u32[]{:S(2)}, u32[]{:S(2)}) collective-permute-start(bf16[256,256]{1,0:T(8,128)(2,1)S(1)} %get-tuple-element.28), channel_id=1, source_target_pairs={{1,0},{2,1},{3,2},{0,3},{5,4},{6,5},{7,6},{4,7},{9,8},{10,9},{11,1... | collective-permute-start | bytes 393224 | tf_op jit(solution)/shard_map/ppermute | solution.py:274
  78.3 3.9 %collective-permute-done.refs_0_ = bf16[256,256]{1,0:T(8,128)(2,1)S(1)} collective-permute-done((bf16[256,256]{1,0:T(8,128)(2,1)S(1)}, bf16[256,256]{1,0:T(8,128)(2,1)S(1)}, u32[]{:S(2)}, u32[]{:S(2)}) %collective-permute-start) | collective-permute-done | bytes 131104 | tf_op jit(solution)/shard_map/ppermute | solution.py:273
  82.2 0.4 collective-permute-done.1.refs_2_
  82.7 0.0 copy-start.7
  82.7 1.0 copy-done.7
  83.7 0.0 copy-start.9
  83.7 1.0 copy-done.9
  84.8 5.1 %conv_backward.4 = (bf16[1024,256]{1,0:T(8,128)(2,1)S(1)}, bf16[9,256,256]{2,1,0:T(8,128)(2,1)S(1)}) custom-call(bf16[256,256]{1,0:T(8,128)(2,1)S(1)} %collective-permute-done.refs_0_, bf16[1024,256]{1,0:T(8,128)(2,1)S(1)} %copy-done.7, bf16[256,256]{1,0:T(8,128)(2,1)S(1)} %collective-permute-done.1.refs_2_, s32[1,256]{1,0:T(1,128)S(1)} %get-tuple-element.32.refs_3_, ...), custom_call_target="tpu_custom_call" | custom-call | flops 2415919104 | bytes 8388608 | tf_op jit(solution)/shard_map/conv_backward/pallas_call | solution.py:198
  89.9 0.0 copy-start.2
  89.9 1.0 copy-done.2
  90.9 0.8 copy-done.4
  91.7 0.0 reduce-scatter.6.cloned.1.call-update
  91.8 0.0 reduce-scatter.4.cloned.1.call-start
  91.8 1.0 fusion.23
  92.8 1.3 collective-permute-start.2
  94.1 1.7 collective-permute-start.3
  95.8 3.1 %collective-permute-done.2.refs_0_ = bf16[256,256]{1,0:T(8,128)(2,1)S(1)} collective-permute-done((bf16[256,256]{1,0:T(8,128)(2,1)S(1)}, bf16[256,256]{1,0:T(8,128)(2,1)S(1)}, u32[]{:S(2)}, u32[]{:S(2)}) %collective-permute-start.2) | collective-permute-done | bytes 131104 | tf_op jit(solution)/shard_map/ppermute | solution.py:273
  98.9 4.2 %collective-permute-done.3.refs_2_ = bf16[256,256]{1,0:T(8,128)(2,1)S(1)} collective-permute-done((bf16[256,256]{1,0:T(8,128)(2,1)S(1)}, bf16[256,256]{1,0:T(8,128)(2,1)S(1)}, u32[]{:S(2)}, u32[]{:S(2)}) %collective-permute-start.3) | collective-permute-done | bytes 131104 | tf_op jit(solution)/shard_map/ppermute | solution.py:274
  103.1 1.0 copy-done.5
  104.2 1.0 copy-done.10
  105.2 5.9 %conv_backward.5 = (bf16[256,1024]{1,0:T(8,128)(2,1)}, bf16[9,256,256]{2,1,0:T(8,128)(2,1)}) custom-call(bf16[256,256]{1,0:T(8,128)(2,1)S(1)} %collective-permute-done.2.refs_0_, bf16[1024,256]{1,0:T(8,128)(2,1)S(1)} %copy-done.5, bf16[256,256]{1,0:T(8,128)(2,1)S(1)} %collective-permute-done.3.refs_2_, s32[1,256]{1,0:T(1,128)S(1)} %get-tuple-element.30.refs_3_, ...), custom_call_target="tpu_custom_call" | custom-call | flops 2415919104 | bytes 8388608 | tf_op jit(solution)/shard_map/conv_backward/pallas_call | solution.py:198
  111.1 0.0 reduce-scatter.4.cloned.1.call-update
  111.2 0.0 all-reduce.3.cloned.1.call-start
  111.2 0.0 reduce-scatter.8.cloned.1.call-done
  111.2 25.0 %reduce-scatter.6.cloned.1.call-done = bf16[9,64,256]{2,1,0:T(8,128)(2,1)} async-done(((bf16[9,256,256]{2,1,0:T(8,128)(2,1)}), bf16[9,64,256]{2,1,0:T(8,128)(2,1)}) %reduce-scatter.6.cloned.1.call-update) | async-done | bytes 294928 | tf_op jit(solution)/shard_map/reduce_scatter | solution.py:270
  136.3 32.1 %reduce-scatter.4.cloned.1.call-done = bf16[9,64,256]{2,1,0:T(8,128)(2,1)} async-done(((bf16[9,256,256]{2,1,0:T(8,128)(2,1)}), bf16[9,64,256]{2,1,0:T(8,128)(2,1)}) %reduce-scatter.4.cloned.1.call-update) | async-done | bytes 294928 | tf_op jit(solution)/shard_map/reduce_scatter | solution.py:270
  168.3 0.0 all-reduce.3.cloned.1.call-update
  168.4 59.9 %all-reduce.3.cloned.1.call-done = (bf16[1,9,64,256]{3,2,1,0:T(8,128)(2,1)}, bf16[1,9,64,256]{3,2,1,0:T(8,128)(2,1)}, bf16[1,9,64,256]{3,2,1,0:T(8,128)(2,1)}) async-done(((bf16[1,9,64,256]{3,2,1,0:T(8,128)(2,1)}, bf16[1,9,64,256]{3,2,1,0:T(8,128)(2,1)}, bf16[1,9,64,256]{3,2,1,0:T(8,128)(2,1)}), (bf16[1,9,64,256]{3,2,1,0:T(8,128)(2,1)}, bf16[1,9,64,256]{3,2,1,0:T(8,128)(2,1)}, ...) | async-done | bytes 884752 | tf_op jit(solution)/shard_map/psum | solution.py:271
  228.2 2.5 %maximum_convert_fusion = f32[3,9,64,256]{3,2,1,0:T(8,128)} fusion(bf16[1,9,64,256]{3,2,1,0:T(8,128)(2,1)} %get-tuple-element.18, bf16[1,9,64,256]{3,2,1,0:T(8,128)(2,1)} %get-tuple-element.19, bf16[1,9,64,256]{3,2,1,0:T(8,128)(2,1)} %get-tuple-element.20), kind=kLoop, calls=%fused_computation.15 | loop fusion | flops 1327104 | bytes 2654208 | tf_op jit(solution)/shard_map/stack | solution.py:276
  (8 shorter events, 0.1 us)
Async XLA Ops:
  7.2 1.2 copy-start
  7.2 104.0 %reduce-scatter.8.cloned.1.call-start = ((), (), s32[]{:S(2)}) async-start(), calls=%async_computation.5 | async-start | bytes 1474560 | tf_op jit(solution)/shard_map/reduce_scatter | solution.py:270
  10.1 2.3 copy-start.13
  10.1 2.3 copy-start.3
  10.1 31.3 %copy-start.12 = (bf16[256,256]{1,0:T(8,128)(2,1)S(1)}, bf16[256,256]{1,0:T(8,128)(2,1)}, u32[]{:S(2)}) copy-start(bf16[256,256]{1,0:T(8,128)(2,1)} %param.11) | copy-start | bytes 393220
  45.1 4.5 %copy-start.11 = (f32[64,64,64]{2,0,1:T(8,128)S(1)}, f32[64,64,64]{2,0,1:T(8,128)}, u32[]{:S(2)}) copy-start(f32[64,64,64]{2,0,1:T(8,128)} %get-tuple-element.21) | copy-start | bytes 3145732
  64.9 2.3 copy-start.14
  64.9 2.4 copy-start.8
  72.4 1.0 copy-start.1
  73.5 0.8 copy-start.6
  74.3 62.0 %reduce-scatter.6.cloned.1.call-start = ((), (), s32[]{:S(2)}) async-start(), calls=%async_computation.4 | async-start | bytes 1474560 | tf_op jit(solution)/shard_map/reduce_scatter | solution.py:270
  75.3 6.9 %collective-permute-start = (bf16[256,256]{1,0:T(8,128)(2,1)S(1)}, bf16[256,256]{1,0:T(8,128)(2,1)S(1)}, u32[]{:S(2)}, u32[]{:S(2)}) collective-permute-start(bf16[256,256]{1,0:T(8,128)(2,1)S(1)} %get-tuple-element.29), channel_id=1, source_target_pairs={{0,1},{1,2},{2,3},{3,0},{4,5},{5,6},{6,7},{7,4},{8,9},{9,10},{10,1... | collective-permute-start | bytes 393224 | tf_op jit(solution)/shard_map/ppermute | solution.py:273
  75.9 6.8 %collective-permute-start.1 = (bf16[256,256]{1,0:T(8,128)(2,1)S(1)}, bf16[256,256]{1,0:T(8,128)(2,1)S(1)}, u32[]{:S(2)}, u32[]{:S(2)}) collective-permute-start(bf16[256,256]{1,0:T(8,128)(2,1)S(1)} %get-tuple-element.28), channel_id=1, source_target_pairs={{1,0},{2,1},{3,2},{0,3},{5,4},{6,5},{7,6},{4,7},{9,8},{10,9},{11,1... | collective-permute-start | bytes 393224 | tf_op jit(solution)/shard_map/ppermute | solution.py:274
  82.7 1.0 copy-start.7
  83.7 1.0 copy-start.9
  89.9 1.0 copy-start.2
  90.9 0.8 copy-start.4
  91.8 76.6 %reduce-scatter.4.cloned.1.call-start = ((), (), s32[]{:S(2)}) async-start(), calls=%async_computation.3 | async-start | bytes 1474560 | tf_op jit(solution)/shard_map/reduce_scatter | solution.py:270
  92.8 6.1 %collective-permute-start.2 = (bf16[256,256]{1,0:T(8,128)(2,1)S(1)}, bf16[256,256]{1,0:T(8,128)(2,1)S(1)}, u32[]{:S(2)}, u32[]{:S(2)}) collective-permute-start(bf16[256,256]{1,0:T(8,128)(2,1)S(1)} %get-tuple-element.27), channel_id=1, source_target_pairs={{0,1},{1,2},{2,3},{3,0},{4,5},{5,6},{6,7},{7,4},{8,9},{9,10},{10,1... | collective-permute-start | bytes 393224 | tf_op jit(solution)/shard_map/ppermute | solution.py:273
  94.1 9.0 %collective-permute-start.3 = (bf16[256,256]{1,0:T(8,128)(2,1)S(1)}, bf16[256,256]{1,0:T(8,128)(2,1)S(1)}, u32[]{:S(2)}, u32[]{:S(2)}) collective-permute-start(bf16[256,256]{1,0:T(8,128)(2,1)S(1)} %get-tuple-element.26), channel_id=1, source_target_pairs={{1,0},{2,1},{3,2},{0,3},{5,4},{6,5},{7,6},{4,7},{9,8},{10,9},{11,1... | collective-permute-start | bytes 393224 | tf_op jit(solution)/shard_map/ppermute | solution.py:274
  103.1 1.0 copy-start.5
  104.2 1.0 copy-start.10
  111.2 117.1 %all-reduce.3.cloned.1.call-start = ((), (), s32[]{:S(2)}) async-start(), calls=%async_computation.6 | async-start | bytes 1769472 | tf_op jit(solution)/shard_map/psum | solution.py:271
Sparse Core Ops, SparseCore 0:
  74.4 30.1 reduce-scatter.7
  107.5 28.7 reduce-scatter.5
  139.8 28.5 reduce-scatter.3
  170.8 57.3 all-reduce.2

commit v2 on v1

--- a/solution.py
+++ b/solution.py
@@ -213,6 +213,155 @@
         ),
         name="conv_backward",
     )(*parts, dil, saved, weight)
+
+
+def reduce_kernel(m, nz, *refs):
+    parts, out = refs[:LAYERS], refs[LAYERS]
+    pair_in, pair_sum, chan_in, chan_sum, z_in, z_sum, full = refs[LAYERS + 1 : LAYERS + 8]
+    sems = refs[LAYERS + 8 :]
+    taps, _, width = pair_in.shape[1:]
+    block, share = chan_sum.shape[2], z_sum.shape[1]
+    me = lax.axis_index("chan")
+    samp = lax.axis_index("samp")
+    core, z = lax.rem(samp, 2), lax.div(samp, 2)
+    pair = {"samp": 2 * z + 1 - core}
+    chans = [lax.rem(me + off, m) for off in range(1, m)]
+    zs = [lax.rem(z + off, nz) for off in range(1, nz)]
+    barrier = pltpu.get_barrier_semaphore()
+    peers = [pair] + [{"chan": c} for c in chans] + [{"samp": 2 * k + core} for k in zs]
+    for peer in peers:
+        pl.semaphore_signal(barrier, inc=1, device_id=peer, device_id_type=MESH)
+    pl.semaphore_wait(barrier, len(peers))
+
+    def send(src, dst, sem, place, peer):
+        copy = pltpu.make_async_remote_copy(
+            src_ref=src, dst_ref=dst, send_sem=sem[0].at[place], recv_sem=sem[1].at[place],
+            device_id=peer, device_id_type=MESH,
+        )
+        copy.start()
+        return copy
+
+    def lanes(k):
+        return pl.ds(pl.multiple_of(k * width, width), width)
+
+    def rows(k):
+        return pl.ds(pl.multiple_of(k * block, block), block)
+
+    f32 = jnp.float32
+    order = range(LAYERS - 1, -1, -1)
+    sent = []
+    stage = {}
+    for l in order:
+        stage[l] = [
+            send(parts[l].at[:, :, lanes(1 - core)], pair_in.at[l], sems[0:2], l, pair)
+        ]
+        sent += stage[l]
+    for l in order:
+        for copy in stage[l]:
+            copy.wait_recv()
+
+        def add_pair(t, carry, l=l):
+            total = parts[l][t, :, lanes(core)].astype(f32) + pair_in[l, t].astype(f32)
+            pair_sum[l, t] = total.astype(jnp.bfloat16)
+            return carry
+
+        lax.fori_loop(0, taps, add_pair, 0)
+        stage[l] = [
+            send(
+                pair_sum.at[l, :, rows(c), :], chan_in.at[l, off], sems[2:4], (l, off),
+                {"chan": c},
+            )
+            for off, c in enumerate(chans)
+        ]
+        sent += stage[l]
+    for l in order:
+        for copy in stage[l]:
+            copy.wait_recv()
+
+        def add_chan(t, carry, l=l):
+            total = pair_sum[l, t, rows(me), :].astype(f32)
+            for off in range(m - 1):
+                total = total + chan_in[l, off, t].astype(f32)
+            chan_sum[l, t] = total.astype(jnp.bfloat16)
+            return carry
+
+        lax.fori_loop(0, taps, add_chan, 0)
+        for t in range(taps, nz * share):
+            chan_sum[l, t] = jnp.zeros((block, width), jnp.bfloat16)
+        stage[l] = [
+            send(
+                chan_sum.at[l, pl.ds(k * share, share)], z_in.at[l, off], sems[4:6], (l, off),
+                {"samp": 2 * k + core},
+            )
+            for off, k in enumerate(zs)
+        ]
+        sent += stage[l]
+    for l in order:
+        for copy in stage[l]:
+            copy.wait_recv()
+        for t in range(share):
+            total = chan_sum[l, z * share + t].astype(f32)
+            for off in range(nz - 1):
+                total = total + z_in[l, off, t].astype(f32)
+            z_sum[l, t] = total.astype(jnp.bfloat16)
+            full[l, core, z * share + t] = total.astype(jnp.bfloat16)
+        place = pl.ds(z * share, share)
+        stage[l] = [
+            send(
+                z_sum.at[l], full.at[l, core, place], sems[6:8], (l, off),
+                {"samp": 2 * k + core},
+            )
+            for off, k in enumerate(zs)
+        ]
+        sent += stage[l]
+    for l in order:
+        for copy in stage[l]:
+            copy.wait_recv()
+        stage[l] = [send(full.at[l, core], full.at[l, core], sems[8:10], l, pair)]
+        sent += stage[l]
+    for l in order:
+        for copy in stage[l]:
+            copy.wait_recv()
+
+        def widen(t, carry, l=l):
+            for k in range(2):
+                out[l, t, :, k * width : (k + 1) * width] = full[l, k, t].astype(f32)
+            return carry
+
+        lax.fori_loop(0, taps, widen, 0)
+    for copy in sent:
+        copy.wait_send()
+
+
+def reduce_grads(m, samples, grads):
+    taps, chans, width = grads[0].shape
+    nz, half, block = samples // 2, width // 2, chans // m
+    share = -(-taps // nz)
+    dma, bf16 = pltpu.SemaphoreType.DMA, jnp.bfloat16
+    return pl.pallas_call(
+        functools.partial(reduce_kernel, m, nz),
+        out_shape=jax.ShapeDtypeStruct((LAYERS, taps, block, width), jnp.float32),
+        in_specs=[VMEM] * LAYERS,
+        out_specs=VMEM,
+        scratch_shapes=[
+            pltpu.VMEM((LAYERS, taps, chans, half), bf16),
+            pltpu.VMEM((LAYERS, taps, chans, half), bf16),
+            pltpu.VMEM((LAYERS, m - 1, taps, block, half), bf16),
+            pltpu.VMEM((LAYERS, nz * share, block, half), bf16),
+            pltpu.VMEM((LAYERS, nz - 1, share, block, half), bf16),
+            pltpu.VMEM((LAYERS, share, block, half), bf16),
+            pltpu.VMEM((LAYERS, 2, nz * share, block, half), bf16),
+            dma((LAYERS,)), dma((LAYERS,)),
+            dma((LAYERS, m - 1)), dma((LAYERS, m - 1)),
+            dma((LAYERS, nz - 1)), dma((LAYERS, nz - 1)),
+            dma((LAYERS, nz - 1)), dma((LAYERS, nz - 1)),
+            dma((LAYERS,)), dma((LAYERS,)),
+        ],
+        compiler_params=pltpu.CompilerParams(
+            collective_id=2, has_side_effects=True, vmem_limit_bytes=VMEM_LIMIT
+        ),
+        name="reduce_grads",
+    )(*grads)
 
 
 def on_device(
@@ -267,13 +416,13 @@
         result, local_grad = layer(
             level, norm, parts, dilation[level][None, :], saved[level], conv_weight[level]
         )
-        reduced = lax.psum_scatter(local_grad, "chan", scatter_dimension=1, tiled=True)
-        layer_grads[level] = lax.psum(reduced, "samp").astype(jnp.float32)
+        layer_grads[level] = local_grad
         if level > 0:
             before = lax.ppermute(result[slab - HALO :], "chan", up)
             after = lax.ppermute(result[:HALO], "chan", down)
             parts = (before, result, after)
-    return (result[None], jnp.stack(layer_grads))
+    weight_grad = reduce_grads(n, lax.axis_size("samp"), layer_grads)
+    return (result[None], weight_grad)
 
 
 def solution(mesh):

time: 238 us -> 138 us (0.58)
  waiting for transfers between devices: 129 us -> 8.86 us
  Pallas kernels: 57.3 us -> 102 us
  between operations: 14.7 us -> 1.59 us
  local copies, waits for them, and re-layouts: 17.7 us -> 9.24 us
  other arithmetic: 2.51 us -> 0.03 us
    psum x1 -> x0, waiting for transfers between devices: 59.9 us -> none  [on_device(): layer_grads[level] = lax.psum(reduced, 'samp').astype(jnp.float32)]
    reduce_scatter x3 -> x0, waiting for transfers between devices: 57.1 us -> none  [on_device(): lax.psum_scatter(local_grad, 'chan', scatter_dimension=1, tiled=True)]
    pallas_call x0 -> x1, Pallas kernels: none -> 45.4 us  [reduce_grads(): pl.pallas_call(functools.partial(reduce_kernel, m, nz), out_shape=jax.Sha...]
    unnamed x30 -> x19, local copies, waits for them, and re-layouts: 8.21 us -> 1.65 us
    ppermute x2, waiting for transfers between devices: 4.65 us -> 1.83 us  [on_device(): after = lax.ppermute(result[:HALO], 'chan', down)]
    another operation x1 -> x0, other arithmetic: 2.48 us -> none  [on_device(): return (result[None], jnp.stack(layer_grads))]
  transfers between devices with their start and end apart: 8 -> 4, of which waited for: 7 -> 4; matrix products, arithmetic and copies ran while one was open for 1% -> 0% of each run, Pallas kernels for 5% -> 0%
where the time goes in v2:
time: 138 us
  Pallas kernels  102 us (74%)
  matrix products  10.1 us (7%)
  local copies, waits for them, and re-layouts  9.24 us (7%)
  waiting for transfers between devices  8.86 us (6%)
  starting transfers between devices  5.95 us (4%)
  between operations  1.59 us (1%)
    pallas_call x1, Pallas kernels, reduce_grads(): pl.pallas_call(functools.partial(reduce_kernel, m, nz), out_shape=jax.Sha...  45.4 us
    pallas_call x1, Pallas kernels, gather(): pl.pallas_call(functools.partial(gather_kernel, n), out_shape=(jax.ShapeD...  29 us
    pallas_call x3, Pallas kernels, layer(): pl.pallas_call(functools.partial(layer_kernel, level, norm), out_shape=(j...  15.3 us
    pallas_call x1, Pallas kernels, regroup(): pl.pallas_call(functools.partial(regroup_kernel, n), out_shape=jax.ShapeD...  12.2 us
    ppermute x2, waiting for transfers between devices, on_device(): before = lax.ppermute(result[slab - HALO:], 'chan', up)  7.03 us
    dot_general x1, matrix products, on_device(): jnp.einsum('cxX,cxy->cXy', circulant[0], grid_values, precision=high)  4.47 us
    ppermute x2, starting transfers between devices, on_device(): after = lax.ppermute(result[:HALO], 'chan', down)  4.11 us
  transfers between devices with their start and end apart: 4, of which 4 were waited for; matrix products, arithmetic and copies ran while one was open for 0% of the time, Pallas kernels for 0%

profile of v2, /device:TPU:0, one launch (start us, length us, event | category | flops | bytes accessed | tf_op | source)
XLA Modules:
  0.0 137.6 jit_solution(12992855991887272639)
XLA Ops:
  0.6 0.0 copy-start
  1.4 0.4 copy-done
  1.8 1.8 %fusion.5 = f32[2,64,64,64]{3,1,2,0:T(8,128)S(1)} fusion(s32[64,64]{1,0:T(8,128)S(1)} %add_select_fusion, f32[2,12,64,64]{3,2,1,0:T(8,128)S(1)} %copy-done, s32[]{:T(128)S(6)} %select_n.22), kind=kOutput, calls=%fused_computation.9 | convolution fusion | flops 402915328 | bytes 2195460 | tf_op jit(solution)/shard_map/aci,ixy->acxy/dot_general | solution.py:398
  3.6 0.0 copy-start.7
  3.6 0.0 copy-start.1
  3.6 0.0 copy-start.6
  3.6 2.3 %slice_bitcast_fusion = (f32[64,64,64]{2,0,1:T(8,128)}, f32[64,64,64]{2,0,1:T(8,128)}) fusion(f32[2,64,64,64]{3,1,2,0:T(8,128)S(1)} %fusion.5), kind=kLoop, calls=%fused_computation | loop fusion | bytes 4194304 | tf_op jit(solution)/shard_map/squeeze | solution.py:404
  5.9 0.0 copy-done.7
  5.9 0.0 copy-done.1
  5.9 29.0 %gather_blocks.1 = (bf16[256,4096]{1,0:T(8,128)(2,1)S(1)}, f32[4,8,1024]{2,1,0:T(8,128)S(1)}) custom-call(bf16[64,4096]{1,0:T(8,128)(2,1)S(1)} %bitcast.32, f32[8,1024]{1,0:T(8,128)S(1)} %broadcast_in_dim.25.g_ref), custom_call_target="tpu_custom_call" | custom-call | tf_op jit(solution)/shard_map/gather_blocks/pallas_call | solution.py:62
  34.9 0.0 copy-done.6
  34.9 1.6 %fusion.14 = f32[64,4096]{1,0:T(8,128)} fusion(bf16[256,4096]{1,0:T(8,128)(2,1)S(1)} %get-tuple-element.10, bf16[256,256]{1,0:T(8,128)(2,1)S(1)} %copy-done.6, s32[]{:T(128)S(6)} %select_n.24), kind=kOutput, calls=%fused_computation.16 | convolution fusion | flops 134217728 | bytes 3211268 | tf_op jit(solution)/shard_map/oc,on->cn/dot_general | solution.py:390
  36.4 2.0 %reshape.34 = f32[64,64,64]{2,1,0:T(8,128)S(1)} reshape(f32[64,4096]{1,0:T(8,128)} %fusion.14) | data formatting | bytes 2097152 | tf_op jit(solution)/shard_map/reshape | solution.py:401
  38.5 0.1 mul.14
  38.6 0.0 copy-start.5
  38.6 4.5 %fusion = f32[64,64,64]{2,1,0:T(8,128)S(1)} fusion(f32[64,64,64]{2,1,0:T(8,128)S(1)} %reshape.34, f32[64,64,64]{2,0,1:T(8,128)} %get-tuple-element.19), kind=kOutput, calls=%fused_computation.2 | convolution fusion | flops 100663296 | bytes 3145728 | tf_op jit(solution)/shard_map/cxX,cxy->cXy/dot_general | solution.py:403
  43.1 0.0 copy-done.5
  43.1 2.3 %multiply_convert_fusion = bf16[64,64,64]{2,1,0:T(8,128)(2,1)S(1)} fusion(f32[64,64,64]{2,1,0:T(8,128)S(1)} %fusion, f32[64,64,64]{2,0,1:T(8,128)S(1)} %copy-done.5, f32[64,64]{1,0:T(8,128)S(1)} %mul.14), kind=kOutput, calls=%fused_computation.6 | convolution fusion | flops 101711872 | bytes 2637824 | tf_op jit(solution)/shard_map/cXy,cyY->cXY/dot_general | solution.py:404
  45.4 0.8 reshape.35.x_ref
  46.2 12.2 %regroup_rows.1.refs_0_ = bf16[256,1536]{1,0:T(8,128)(2,1)S(1)} custom-call(bf16[64,4096]{1,0:T(8,128)(2,1)S(1)} %reshape.35.x_ref), custom_call_target="tpu_custom_call" | custom-call | tf_op jit(solution)/shard_map/regroup_rows/pallas_call | solution.py:109
  58.4 0.0 copy-start.8
  58.4 0.0 copy-start.2
  58.4 2.3 %slice_bitcast_fusion.2 = (bf16[9,256,256]{2,1,0:T(8,128)(2,1)S(1)}, bf16[9,256,256]{2,1,0:T(8,128)(2,1)S(1)}, bf16[9,256,256]{2,1,0:T(8,128)(2,1)S(1)}) fusion(bf16[3,9,256,256]{3,2,1,0:T(8,128)(2,1)} %param.18), kind=kLoop, calls=%fused_computation.11 | loop fusion | bytes 7077888 | tf_op jit(solution)/shard_map/squeeze | solution.py:417
  60.8 0.0 copy-done.8
  60.8 0.0 copy-done.2
  60.8 0.0 copy-start.3
  60.8 5.2 %conv_backward.3 = (bf16[1024,256]{1,0:T(8,128)(2,1)S(1)}, bf16[9,256,256]{2,1,0:T(8,128)(2,1)S(1)}) custom-call(bf16[256,1536]{1,0:T(8,128)(2,1)S(1)} %regroup_rows.1.refs_0_, s32[1,256]{1,0:T(1,128)S(1)} %get-tuple-element.28.refs_1_, bf16[256,1024]{1,0:T(8,128)(2,1)S(1)} %bitcast.33, bf16[9,256,256]{2,1,0:T(8,128)(2,1)S(1)} %get-tuple-element.21.refs_3_), custom_call_target="tpu_custom_call" | custom-call | flops 2415919104 | bytes 8388608 | tf_op jit(solution)/shard_map/conv_backward/pallas_call | solution.py:198
  66.0 0.6 collective-permute-start
  66.6 2.4 %collective-permute-start.1 = (bf16[256,256]{1,0:T(8,128)(2,1)S(1)}, bf16[256,256]{1,0:T(8,128)(2,1)S(1)}, u32[]{:S(2)}, u32[]{:S(2)}) collective-permute-start(bf16[256,256]{1,0:T(8,128)(2,1)S(1)} %get-tuple-element.25), channel_id=1, source_target_pairs={{1,0},{2,1},{3,2},{0,3},{5,4},{6,5},{7,6},{4,7},{9,8},{10,9},{11,1... | collective-permute-start | bytes 393224 | tf_op jit(solution)/shard_map/ppermute | solution.py:422
  69.0 3.9 %collective-permute-done.refs_0_ = bf16[256,256]{1,0:T(8,128)(2,1)S(1)} collective-permute-done((bf16[256,256]{1,0:T(8,128)(2,1)S(1)}, bf16[256,256]{1,0:T(8,128)(2,1)S(1)}, u32[]{:S(2)}, u32[]{:S(2)}) %collective-permute-start) | collective-permute-done | bytes 131104 | tf_op jit(solution)/shard_map/ppermute | solution.py:421
  72.9 0.5 collective-permute-done.1.refs_2_
  73.4 0.0 copy-done.3
  73.4 0.0 copy-start.4
  73.4 5.2 %conv_backward.4 = (bf16[1024,256]{1,0:T(8,128)(2,1)S(1)}, bf16[9,256,256]{2,1,0:T(8,128)(2,1)S(1)}) custom-call(bf16[256,256]{1,0:T(8,128)(2,1)S(1)} %collective-permute-done.refs_0_, bf16[1024,256]{1,0:T(8,128)(2,1)S(1)} %get-tuple-element.12.refs_1_, bf16[256,256]{1,0:T(8,128)(2,1)S(1)} %collective-permute-done.1.refs_2_, ...), custom_call_target="tpu_custom_call" | custom-call | flops 2415919104 | bytes 8388608 | tf_op jit(solution)/shard_map/conv_backward/pallas_call | solution.py:198
  78.6 1.3 collective-permute-start.2
  79.9 1.7 %collective-permute-start.3 = (bf16[256,256]{1,0:T(8,128)(2,1)S(1)}, bf16[256,256]{1,0:T(8,128)(2,1)S(1)}, u32[]{:S(2)}, u32[]{:S(2)}) collective-permute-start(bf16[256,256]{1,0:T(8,128)(2,1)S(1)} %get-tuple-element.23), channel_id=1, source_target_pairs={{1,0},{2,1},{3,2},{0,3},{5,4},{6,5},{7,6},{4,7},{9,8},{10,9},{11,1... | collective-permute-start | bytes 393224 | tf_op jit(solution)/shard_map/ppermute | solution.py:422
  81.6 3.1 %collective-permute-done.2.refs_0_ = bf16[256,256]{1,0:T(8,128)(2,1)S(1)} collective-permute-done((bf16[256,256]{1,0:T(8,128)(2,1)S(1)}, bf16[256,256]{1,0:T(8,128)(2,1)S(1)}, u32[]{:S(2)}, u32[]{:S(2)}) %collective-permute-start.2) | collective-permute-done | bytes 131104 | tf_op jit(solution)/shard_map/ppermute | solution.py:421
  84.7 1.4 collective-permute-done.3.refs_2_
  86.0 0.0 copy-done.4
  86.0 4.9 %conv_backward.5 = (bf16[256,1024]{1,0:T(8,128)(2,1)}, bf16[9,256,256]{2,1,0:T(8,128)(2,1)S(1)}) custom-call(bf16[256,256]{1,0:T(8,128)(2,1)S(1)} %collective-permute-done.2.refs_0_, bf16[1024,256]{1,0:T(8,128)(2,1)S(1)} %get-tuple-element.13.refs_1_, bf16[256,256]{1,0:T(8,128)(2,1)S(1)} %collective-permute-done.3.refs_2_, ...), custom_call_target="tpu_custom_call" | custom-call | flops 2415919104 | bytes 8388608 | tf_op jit(solution)/shard_map/conv_backward/pallas_call | solution.py:198
  91.0 45.4 %reduce_grads.1 = f32[3,9,64,256]{3,2,1,0:T(8,128)S(1)} custom-call(bf16[9,256,256]{2,1,0:T(8,128)(2,1)S(1)} %get-tuple-element.15.refs_0_, bf16[9,256,256]{2,1,0:T(8,128)(2,1)S(1)} %get-tuple-element.16.refs_1_, bf16[9,256,256]{2,1,0:T(8,128)(2,1)S(1)} %get-tuple-element.17.refs_2_), custom_call_target="tpu_custom_call" | custom-call | tf_op jit(solution)/shard_map/reduce_grads/pallas_call | solution.py:341
  136.4 1.2 copy.25
  (7 shorter events, 0.1 us)
Async XLA Ops:
  0.6 1.2 copy-start
  3.6 2.3 %copy-start.7 = (s32[1,1024]{1,0:T(1,128)S(1)}, s32[1,1024]{1,0:T(1,128)}, u32[]{:S(2)}) copy-start(s32[1,1024]{1,0:T(1,128)} %param.14) | copy-start | bytes 12292
  3.6 2.3 %copy-start.1 = (bf16[1,64,4096]{2,1,0:T(8,128)(2,1)S(1)}, bf16[1,64,4096]{2,1,0:T(8,128)(2,1)}, u32[]{:S(2)}) copy-start(bf16[1,64,4096]{2,1,0:T(8,128)(2,1)} %param.10) | copy-start | bytes 1572868
  3.6 31.3 %copy-start.6 = (bf16[256,256]{1,0:T(8,128)(2,1)S(1)}, bf16[256,256]{1,0:T(8,128)(2,1)}, u32[]{:S(2)}) copy-start(bf16[256,256]{1,0:T(8,128)(2,1)} %param.11) | copy-start | bytes 393220
  38.6 4.5 %copy-start.5 = (f32[64,64,64]{2,0,1:T(8,128)S(1)}, f32[64,64,64]{2,0,1:T(8,128)}, u32[]{:S(2)}) copy-start(f32[64,64,64]{2,0,1:T(8,128)} %get-tuple-element.18) | copy-start | bytes 3145732
  58.4 2.4 %copy-start.8 = (s32[3,256]{1,0:T(4,128)S(1)}, s32[3,256]{1,0:T(4,128)}, u32[]{:S(2)}) copy-start(s32[3,256]{1,0:T(4,128)} %param.19) | copy-start | bytes 9220
  58.4 2.4 %copy-start.2 = (bf16[1,256,1024]{2,1,0:T(8,128)(2,1)S(1)}, bf16[1,256,1024]{2,1,0:T(8,128)(2,1)}, u32[]{:S(2)}) copy-start(bf16[1,256,1024]{2,1,0:T(8,128)(2,1)} %param.17) | copy-start | bytes 1572868
  60.8 12.6 %copy-start.3 = (bf16[1,256,1024]{2,1,0:T(8,128)(2,1)S(1)}, bf16[1,256,1024]{2,1,0:T(8,128)(2,1)}, u32[]{:S(2)}) copy-start(bf16[1,256,1024]{2,1,0:T(8,128)(2,1)} %param.16) | copy-start | bytes 1572868
  66.0 6.9 %collective-permute-start = (bf16[256,256]{1,0:T(8,128)(2,1)S(1)}, bf16[256,256]{1,0:T(8,128)(2,1)S(1)}, u32[]{:S(2)}, u32[]{:S(2)}) collective-permute-start(bf16[256,256]{1,0:T(8,128)(2,1)S(1)} %get-tuple-element.26), channel_id=1, source_target_pairs={{0,1},{1,2},{2,3},{3,0},{4,5},{5,6},{6,7},{7,4},{8,9},{9,10},{10,1... | collective-permute-start | bytes 393224 | tf_op jit(solution)/shard_map/ppermute | solution.py:421
  66.6 6.8 %collective-permute-start.1 = (bf16[256,256]{1,0:T(8,128)(2,1)S(1)}, bf16[256,256]{1,0:T(8,128)(2,1)S(1)}, u32[]{:S(2)}, u32[]{:S(2)}) collective-permute-start(bf16[256,256]{1,0:T(8,128)(2,1)S(1)} %get-tuple-element.25), channel_id=1, source_target_pairs={{1,0},{2,1},{3,2},{0,3},{5,4},{6,5},{7,6},{4,7},{9,8},{10,9},{11,1... | collective-permute-start | bytes 393224 | tf_op jit(solution)/shard_map/ppermute | solution.py:422
  73.4 12.7 %copy-start.4 = (bf16[1,256,1024]{2,1,0:T(8,128)(2,1)S(1)}, bf16[1,256,1024]{2,1,0:T(8,128)(2,1)}, u32[]{:S(2)}) copy-start(bf16[1,256,1024]{2,1,0:T(8,128)(2,1)} %param.15) | copy-start | bytes 1572868
  78.6 6.1 %collective-permute-start.2 = (bf16[256,256]{1,0:T(8,128)(2,1)S(1)}, bf16[256,256]{1,0:T(8,128)(2,1)S(1)}, u32[]{:S(2)}, u32[]{:S(2)}) collective-permute-start(bf16[256,256]{1,0:T(8,128)(2,1)S(1)} %get-tuple-element.24), channel_id=1, source_target_pairs={{0,1},{1,2},{2,3},{3,0},{4,5},{5,6},{6,7},{7,4},{8,9},{9,10},{10,1... | collective-permute-start | bytes 393224 | tf_op jit(solution)/shard_map/ppermute | solution.py:421
  79.9 6.2 %collective-permute-start.3 = (bf16[256,256]{1,0:T(8,128)(2,1)S(1)}, bf16[256,256]{1,0:T(8,128)(2,1)S(1)}, u32[]{:S(2)}, u32[]{:S(2)}) collective-permute-start(bf16[256,256]{1,0:T(8,128)(2,1)S(1)} %get-tuple-element.23), channel_id=1, source_target_pairs={{1,0},{2,1},{3,2},{0,3},{5,4},{6,5},{7,6},{4,7},{9,8},{10,9},{11,1... | collective-permute-start | bytes 393224 | tf_op jit(solution)/shard_map/ppermute | solution.py:422

commit v3 on v1

--- a/solution.py
+++ b/solution.py
@@ -119,100 +119,255 @@
     )(x)
 
 
-def layer_kernel(level, norm, *refs):
-    if level == LAYERS - 1:
-        padded, dil, saved, weight, out, grads, col, taps = refs
-    else:
-        before, inner, after, dil, saved, weight, out, grads, col, taps = refs
-    chans = weight.shape[1]
-    cells = saved.shape[1]
-    rows = cells // SIDE
-    if level == LAYERS - 1:
-        for start in range(0, cells + 2 * HALO, 256):
-            block = padded[:, start : start + 256].astype(jnp.float32)
-            col[1, start : start + 256, :] = block.T.astype(jnp.bfloat16)
-    else:
-        col[1, :HALO, :] = before[...]
-        col[1, HALO : HALO + cells, :] = inner[...]
-        col[1, HALO + cells :, :] = after[...]
-    step = dil[...]
-
-    def shift_columns(r, carry):
-        at = pl.ds(pl.multiple_of(r * SIDE, SIDE), SIDE)
-        value = col[1, at, :].astype(jnp.float32)
-        for sign in (-1, 1):
-            chosen = pltpu.roll(value, sign % SIDE, 0)
-            for d in range(2, MAXDIL + 1):
-                chosen = jnp.where(step == d, pltpu.roll(value, (sign * d) % SIDE, 0), chosen)
-            col[sign + 1, at, :] = chosen.astype(jnp.bfloat16)
-        return carry
-
-    lax.fori_loop(0, rows + 2 * MAXDIL, shift_columns, 0)
-
-    picks = [(step == d).astype(jnp.float32).astype(jnp.bfloat16) for d in range(1, MAXDIL + 1)]
-
-    def shift_rows(r, carry):
-        at = pl.ds(pl.multiple_of(r * SIDE, SIDE), SIDE)
-        for i in (-1, 0, 1):
-            for j in (-1, 0, 1):
-                tap = 3 * (i + 1) + j + 1
-                if i == 0:
-                    value = col[j + 1, pl.ds(pl.multiple_of((r + MAXDIL) * SIDE, SIDE), SIDE), :]
-                else:
-                    value = None
-                    for d in range(1, MAXDIL + 1):
-                        begin = pl.multiple_of((r + MAXDIL - i * d) * SIDE, SIDE)
-                        term = col[j + 1, pl.ds(begin, SIDE), :] * picks[d - 1]
-                        value = term if value is None else value + term
-                taps[at, tap * chans : (tap + 1) * chans] = value
-        return carry
-
-    lax.fori_loop(0, rows, shift_rows, 0)
-
-    if level == 0:
-        act = saved[...]
-    else:
-        act = jnp.tanh(saved[...].astype(jnp.float32)).astype(jnp.bfloat16)
-    flat_weight = weight[...].reshape(9 * chans, chans)
-    for start in range(0, cells, 256):
-        back = jnp.dot(
-            taps[start : start + 256, :], flat_weight, preferred_element_type=jnp.float32
+def backward_kernel(m, nz, norm, *refs):
+    padded, dil, weight = refs[:3]
+    saved, (out, summed) = refs[3 : 3 + LAYERS], refs[3 + LAYERS : 5 + LAYERS]
+    rest = refs[5 + LAYERS :]
+    col, taps, halo, grads = rest[:4]
+    pair_in, pair_sum, chan_in, chan_sum, z_in, z_sum, full = rest[4:11]
+    sems = rest[11:]
+    f32, bf16 = jnp.float32, jnp.bfloat16
+    tap_count, _, width = pair_in.shape[1:]
+    block, share = chan_sum.shape[2], z_sum.shape[1]
+    chans, cells = weight.shape[2], saved[0].shape[1]
+    side_rows = cells // SIDE
+    me = lax.axis_index("chan")
+    samp = lax.axis_index("samp")
+    core, z = lax.rem(samp, 2), lax.div(samp, 2)
+    pair = {"samp": 2 * z + 1 - core}
+    others = [lax.rem(me + off, m) for off in range(1, m)]
+    zs = [lax.rem(z + off, nz) for off in range(1, nz)]
+    barrier = pltpu.get_barrier_semaphore()
+    peers = [pair] + [{"chan": c} for c in others] + [{"samp": 2 * k + core} for k in zs]
+    for peer in peers:
+        pl.semaphore_signal(barrier, inc=1, device_id=peer, device_id_type=MESH)
+    pl.semaphore_wait(barrier, len(peers))
+
+    def send(src, dst, sem, place, peer):
+        copy = pltpu.make_async_remote_copy(
+            src_ref=src, dst_ref=dst, send_sem=sem[0].at[place], recv_sem=sem[1].at[place],
+            device_id=peer, device_id_type=MESH,
         )
-        if level == 0:
-            out[:, start : start + 256] = back.T.astype(jnp.bfloat16)
+        copy.start()
+        return copy
+
+    def lanes(k):
+        return pl.ds(pl.multiple_of(k * width, width), width)
+
+    def rows(k):
+        return pl.ds(pl.multiple_of(k * block, block), block)
+
+    stage = [[] for _ in range(LAYERS)]
+    sent = []
+
+    def arrived(l):
+        for copy in stage[l]:
+            copy.wait_recv()
+
+    def go(l, copies):
+        stage[l] = copies
+        sent.extend(copies)
+
+    def start_pair(l):
+        src = grads.at[l, :, :, lanes(1 - core)]
+        go(l, [send(src, pair_in.at[l], sems[0:2], l, pair)])
+
+    def pair_to_chan(l):
+        arrived(l)
+
+        def add_pair(t, carry):
+            total = grads[l, t, :, lanes(core)].astype(f32) + pair_in[l, t].astype(f32)
+            pair_sum[l, t] = total.astype(bf16)
+            return carry
+
+        lax.fori_loop(0, tap_count, add_pair, 0)
+        go(l, [
+            send(
+                pair_sum.at[l, :, rows(c), :], chan_in.at[l, off], sems[2:4], (l, off),
+                {"chan": c},
+            )
+            for off, c in enumerate(others)
+        ])
+
+    def chan_to_z(l):
+        arrived(l)
+
+        def add_chan(t, carry):
+            total = pair_sum[l, t, rows(me), :].astype(f32)
+            for off in range(m - 1):
+                total = total + chan_in[l, off, t].astype(f32)
+            chan_sum[l, t] = total.astype(bf16)
+            return carry
+
+        lax.fori_loop(0, tap_count, add_chan, 0)
+        for t in range(tap_count, nz * share):
+            chan_sum[l, t] = jnp.zeros((block, width), bf16)
+        go(l, [
+            send(
+                chan_sum.at[l, pl.ds(k * share, share)], z_in.at[l, off], sems[4:6], (l, off),
+                {"samp": 2 * k + core},
+            )
+            for off, k in enumerate(zs)
+        ])
+
+    def z_to_full(l):
+        arrived(l)
+        for t in range(share):
+            total = chan_sum[l, z * share + t].astype(f32)
+            for off in range(nz - 1):
+                total = total + z_in[l, off, t].astype(f32)
+            z_sum[l, t] = total.astype(bf16)
+            full[l, core, z * share + t] = total.astype(bf16)
+        place = pl.ds(z * share, share)
+        go(l, [
+            send(z_sum.at[l], full.at[l, core, place], sems[6:8], (l, off), {"samp": 2 * k + core})
+            for off, k in enumerate(zs)
+        ])
+
+    def full_to_pair(l):
+        arrived(l)
+        go(l, [send(full.at[l, core], full.at[l, core], sems[8:10], l, pair)])
+
+    def finish(l):
+        arrived(l)
+
+        def widen(t, carry):
+            for k in range(2):
+                summed[l, t, :, k * width : (k + 1) * width] = full[l, k, t].astype(f32)
+            return carry
+
+        lax.fori_loop(0, tap_count, widen, 0)
+
+    edge = []
+    for level in range(LAYERS - 1, -1, -1):
+        if level == LAYERS - 1:
+            for start in range(0, cells + 2 * HALO, 256):
+                piece = padded[:, start : start + 256].astype(f32)
+                col[1, start : start + 256, :] = piece.T.astype(bf16)
         else:
-            slope = jnp.tanh(saved[:, start : start + 256].astype(jnp.float32))
-            slope = 1.0 - slope * slope
-            out[start : start + 256, :] = (back * slope.T).astype(jnp.bfloat16)
-    for tap in range(9):
-        term = jnp.dot(
-            act, taps[:, tap * chans : (tap + 1) * chans], preferred_element_type=jnp.float32
-        )
-        grads[tap] = (term * norm).T.astype(jnp.bfloat16)
-
-
-def layer(level, norm, parts, dil, saved, weight):
-    chans, cells = saved.shape
-    out_dims = (chans, cells) if level == 0 else (cells, chans)
-    flops = 2 * 2 * 9 * chans * chans * cells
+            for copy in edge:
+                copy.wait()
+            col[1, :HALO, :] = halo[level, 0]
+            col[1, HALO + cells :, :] = halo[level, 1]
+        step = dil[level : level + 1, :]
+
+        def shift_columns(r, carry, step=step):
+            at = pl.ds(pl.multiple_of(r * SIDE, SIDE), SIDE)
+            value = col[1, at, :].astype(f32)
+            for sign in (-1, 1):
+                chosen = pltpu.roll(value, sign % SIDE, 0)
+                for d in range(2, MAXDIL + 1):
+                    chosen = jnp.where(step == d, pltpu.roll(value, (sign * d) % SIDE, 0), chosen)
+                col[sign + 1, at, :] = chosen.astype(bf16)
+            return carry
+
+        lax.fori_loop(0, side_rows + 2 * MAXDIL, shift_columns, 0)
+        if level < LAYERS - 1:
+            pair_to_chan(level + 1)
+        picks = [(step == d).astype(f32).astype(bf16) for d in range(1, MAXDIL + 1)]
+
+        def shift_rows(r, carry, picks=picks):
+            at = pl.ds(pl.multiple_of(r * SIDE, SIDE), SIDE)
+            for i in (-1, 0, 1):
+                for j in (-1, 0, 1):
+                    tap = 3 * (i + 1) + j + 1
+                    if i == 0:
+                        begin = pl.multiple_of((r + MAXDIL) * SIDE, SIDE)
+                        value = col[j + 1, pl.ds(begin, SIDE), :]
+                    else:
+                        value = None
+                        for d in range(1, MAXDIL + 1):
+                            begin = pl.multiple_of((r + MAXDIL - i * d) * SIDE, SIDE)
+                            term = col[j + 1, pl.ds(begin, SIDE), :] * picks[d - 1]
+                            value = term if value is None else value + term
+                    taps[at, tap * chans : (tap + 1) * chans] = value
+            return carry
+
+        lax.fori_loop(0, side_rows, shift_rows, 0)
+        flat_weight = weight[level].reshape(tap_count * chans, chans)
+        for start in range(0, cells, 256):
+            back = jnp.dot(taps[start : start + 256, :], flat_weight, preferred_element_type=f32)
+            if level == 0:
+                out[:, start : start + 256] = back.T.astype(bf16)
+            else:
+                slope = jnp.tanh(saved[level][:, start : start + 256].astype(f32))
+                slope = 1.0 - slope * slope
+                col[1, HALO + start : HALO + start + 256, :] = (back * slope.T).astype(bf16)
+        if level > 0:
+            up, down = {"chan": others[0]}, {"chan": others[m - 2]}
+            edge = [
+                send(
+                    col.at[1, pl.ds(cells, HALO), :], halo.at[level - 1, 0],
+                    sems[10:12], (level - 1, 0), up,
+                ),
+                send(
+                    col.at[1, pl.ds(HALO, HALO), :], halo.at[level - 1, 1],
+                    sems[10:12], (level - 1, 1), down,
+                ),
+            ]
+            act = jnp.tanh(saved[level][...].astype(f32)).astype(bf16)
+        else:
+            chan_to_z(LAYERS - 1)
+            act = saved[level][...]
+        for tap in range(tap_count):
+            term = jnp.dot(
+                act, taps[:, tap * chans : (tap + 1) * chans], preferred_element_type=f32
+            )
+            grads[level, tap] = (term * norm).T.astype(bf16)
+        start_pair(level)
+    z_to_full(2)
+    pair_to_chan(0)
+    full_to_pair(2)
+    chan_to_z(1)
+    z_to_full(1)
+    finish(2)
+    chan_to_z(0)
+    full_to_pair(1)
+    z_to_full(0)
+    finish(1)
+    full_to_pair(0)
+    finish(0)
+    for copy in sent:
+        copy.wait_send()
+
+
+def backward(m, samples, norm, padded, dil, weight, saved):
+    chans, cells = saved[0].shape
+    nz, half, block, taps = samples // 2, chans // 2, chans // m, weight.shape[1]
+    share = -(-taps // nz)
+    dma, bf16 = pltpu.SemaphoreType.DMA, jnp.bfloat16
     return pl.pallas_call(
-        functools.partial(layer_kernel, level, norm),
+        functools.partial(backward_kernel, m, nz, norm),
         out_shape=(
-            jax.ShapeDtypeStruct(out_dims, jnp.bfloat16),
-            jax.ShapeDtypeStruct((9, chans, chans), jnp.bfloat16),
+            jax.ShapeDtypeStruct((chans, cells), bf16),
+            jax.ShapeDtypeStruct((LAYERS, taps, block, chans), jnp.float32),
         ),
-        in_specs=[VMEM] * (len(parts) + 3),
+        in_specs=[VMEM] * (3 + LAYERS),
         out_specs=(VMEM, VMEM),
         scratch_shapes=[
-            pltpu.VMEM((3, cells + 2 * HALO, chans), jnp.bfloat16),
-            pltpu.VMEM((cells, 9 * chans), jnp.bfloat16),
+            pltpu.VMEM((3, cells + 2 * HALO, chans), bf16),
+            pltpu.VMEM((cells, taps * chans), bf16),
+            pltpu.VMEM((LAYERS - 1, 2, HALO, chans), bf16),
+            pltpu.VMEM((LAYERS, taps, chans, chans), bf16),
+            pltpu.VMEM((LAYERS, taps, chans, half), bf16),
+            pltpu.VMEM((LAYERS, taps, chans, half), bf16),
+            pltpu.VMEM((LAYERS, m - 1, taps, block, half), bf16),
+            pltpu.VMEM((LAYERS, nz * share, block, half), bf16),
+            pltpu.VMEM((LAYERS, nz - 1, share, block, half), bf16),
+            pltpu.VMEM((LAYERS, share, block, half), bf16),
+            pltpu.VMEM((LAYERS, 2, nz * share, block, half), bf16),
+            dma((LAYERS,)), dma((LAYERS,)),
+            dma((LAYERS, m - 1)), dma((LAYERS, m - 1)),
+            dma((LAYERS, nz - 1)), dma((LAYERS, nz - 1)),
+            dma((LAYERS, nz - 1)), dma((LAYERS, nz - 1)),
+            dma((LAYERS,)), dma((LAYERS,)),
+            dma((LAYERS - 1, 2)), dma((LAYERS - 1, 2)),
         ],
-        compiler_params=pltpu.CompilerParams(vmem_limit_bytes=VMEM_LIMIT),
-        cost_estimate=pl.CostEstimate(
-            flops=flops, bytes_accessed=8 * 1024 * 1024, transcendentals=chans * cells
+        compiler_params=pltpu.CompilerParams(
+            collective_id=2, has_side_effects=True, vmem_limit_bytes=VMEM_LIMIT
         ),
         name="conv_backward",
-    )(*parts, dil, saved, weight)
+    )(padded, dil, weight, *saved)
 
 
 def on_device(
@@ -257,23 +412,11 @@
     gated = (corr_grad * gates).astype(jnp.bfloat16).reshape(chan_block, site_count)
     padded = regroup(n, gated)
     norm = 1.0 / math.sqrt(out_cot.shape[0] * lax.axis_size("samp") * site_count)
-    up = [(i, (i + 1) % n) for i in range(n)]
-    down = [(j, i) for i, j in up]
     saved = (layer_input[0], pre_one[0], pre_two[0])
-    layer_grads = [None] * LAYERS
-    parts = (padded,)
-    result = None
-    for level in range(LAYERS - 1, -1, -1):
-        result, local_grad = layer(
-            level, norm, parts, dilation[level][None, :], saved[level], conv_weight[level]
-        )
-        reduced = lax.psum_scatter(local_grad, "chan", scatter_dimension=1, tiled=True)
-        layer_grads[level] = lax.psum(reduced, "samp").astype(jnp.float32)
-        if level > 0:
-            before = lax.ppermute(result[slab - HALO :], "chan", up)
-            after = lax.ppermute(result[:HALO], "chan", down)
-            parts = (before, result, after)
-    return (result[None], jnp.stack(layer_grads))
+    result, weight_grad = backward(
+        n, lax.axis_size("samp"), norm, padded, dilation, conv_weight, saved
+    )
+    return (result[None], weight_grad)
 
 
 def solution(mesh):

time: 238 us -> 131 us (0.55)
  waiting for transfers between devices: 129 us -> 0 us
  Pallas kernels: 57.3 us -> 108 us
  between operations: 14.7 us -> 1.51 us
  local copies, waits for them, and re-layouts: 17.7 us -> 9.16 us
  starting transfers between devices: 6.12 us -> 0 us
  other arithmetic: 2.51 us -> 0.03 us
    psum x1 -> x0, waiting for transfers between devices: 59.9 us -> none  [on_device(): layer_grads[level] = lax.psum(reduced, 'samp').astype(jnp.float32)]
    reduce_scatter x3 -> x0, waiting for transfers between devices: 57.1 us -> none  [on_device(): lax.psum_scatter(local_grad, 'chan', scatter_dimension=1, tiled=True)]
    pallas_call x3 -> x1, Pallas kernels: 16.2 us -> 67.3 us  [backward(): pl.pallas_call(functools.partial(backward_kernel, m, nz, norm), out_shape...]
    ppermute x4 -> x0, waiting for transfers between devices: 11.7 us -> none  [the longest x2 7.07 us: on_device(): before = lax.ppermute(result[slab - HALO:], 'chan', up)]
    ppermute x4 -> x0, starting transfers between devices: 5.95 us -> none  [the longest x2 4.11 us: on_device(): after = lax.ppermute(result[:HALO], 'chan', down)]
    unnamed x30 -> x18, local copies, waits for them, and re-layouts: 8.21 us -> 2.43 us
    dot_general x1, matrix products: 2.32 us -> 4.8 us  [on_device(): jnp.einsum('cXy,cyY->cXY', halfway, circulant[1], precision=high)]
    another operation x1 -> x0, other arithmetic: 2.48 us -> none  [on_device(): return (result[None], jnp.stack(layer_grads))]
  transfers between devices with their start and end apart: 8 -> 0, of which waited for: 7 -> 0; matrix products, arithmetic and copies ran while one was open for 1% -> 0% of each run, Pallas kernels for 5% -> 0%
where the time goes in v3:
time: 131 us
  Pallas kernels  108 us (82%)
  matrix products  12.1 us (9%)
  local copies, waits for them, and re-layouts  9.16 us (7%)
  between operations  1.51 us (1%)
    pallas_call x1, Pallas kernels, backward(): pl.pallas_call(functools.partial(backward_kernel, m, nz, norm), out_shape...  67.3 us
    pallas_call x1, Pallas kernels, gather(): pl.pallas_call(functools.partial(gather_kernel, n), out_shape=(jax.ShapeD...  29 us
    pallas_call x1, Pallas kernels, regroup(): pl.pallas_call(functools.partial(regroup_kernel, n), out_shape=jax.ShapeD...  12.2 us
    dot_general x1, matrix products, on_device(): jnp.einsum('cxX,cxy->cXy', circulant[0], grid_values, precision=high)  4.91 us
    dot_general x1, matrix products, on_device(): jnp.einsum('cXy,cyY->cXY', halfway, circulant[1], precision=high)  4.8 us

profile of v3, /device:TPU:0, one launch (start us, length us, event | category | flops | bytes accessed | tf_op | source)
XLA Modules:
  0.0 131.2 jit_solution(6789184932869166715)
XLA Ops:
  0.6 0.0 copy-start
  1.4 0.4 copy-done
  1.8 1.8 %fusion.5 = f32[2,64,64,64]{3,1,2,0:T(8,128)S(1)} fusion(s32[64,64]{1,0:T(8,128)S(1)} %add_select_fusion, f32[2,12,64,64]{3,2,1,0:T(8,128)S(1)} %copy-done, s32[]{:T(128)S(6)} %select_n.22), kind=kOutput, calls=%fused_computation.9 | convolution fusion | flops 402915328 | bytes 2195460 | tf_op jit(solution)/shard_map/aci,ixy->acxy/dot_general | solution.py:404
  3.6 0.0 copy-start.7
  3.6 0.0 copy-start.4
  3.6 0.0 copy-start.6
  3.6 2.2 %slice_bitcast_fusion = (f32[64,64,64]{2,0,1:T(8,128)}, f32[64,64,64]{2,0,1:T(8,128)}) fusion(f32[2,64,64,64]{3,1,2,0:T(8,128)S(1)} %fusion.5), kind=kLoop, calls=%fused_computation | loop fusion | bytes 4194304 | tf_op jit(solution)/shard_map/squeeze | solution.py:410
  5.9 0.0 copy-done.7
  5.9 0.0 copy-done.4
  5.9 29.0 %gather_blocks.1 = (bf16[256,4096]{1,0:T(8,128)(2,1)S(1)}, f32[4,8,1024]{2,1,0:T(8,128)S(1)}) custom-call(bf16[64,4096]{1,0:T(8,128)(2,1)S(1)} %bitcast.29, f32[8,1024]{1,0:T(8,128)S(1)} %broadcast_in_dim.25.g_ref), custom_call_target="tpu_custom_call" | custom-call | tf_op jit(solution)/shard_map/gather_blocks/pallas_call | solution.py:62
  34.9 0.0 copy-done.6
  34.9 0.6 fusion.14
  35.5 2.2 %reshape.34 = f32[64,64,64]{2,1,0:T(8,128)} reshape(f32[64,4096]{1,0:T(8,128)S(1)} %fusion.14) | data formatting | bytes 2097152 | tf_op jit(solution)/shard_map/reshape | solution.py:407
  37.6 4.9 %fusion = f32[64,64,64]{2,1,0:T(8,128)S(1)} fusion(f32[64,64,64]{2,1,0:T(8,128)} %reshape.34, f32[64,64,64]{2,0,1:T(8,128)} %get-tuple-element.11), kind=kOutput, calls=%fused_computation.2 | convolution fusion | flops 100663296 | bytes 3145728 | tf_op jit(solution)/shard_map/cxX,cxy->cXy/dot_general | solution.py:409
  42.6 0.1 mul.14
  42.7 4.8 %multiply_convert_fusion = bf16[64,64,64]{2,1,0:T(8,128)(2,1)} fusion(f32[64,64,64]{2,1,0:T(8,128)S(1)} %fusion, f32[64,64,64]{2,0,1:T(8,128)} %get-tuple-element.10, f32[64,64]{1,0:T(8,128)S(1)} %mul.14), kind=kOutput, calls=%fused_computation.6 | convolution fusion | flops 101711872 | bytes 2637824 | tf_op jit(solution)/shard_map/cXy,cyY->cXY/dot_general | solution.py:410
  47.5 0.0 copy-start.1
  47.5 0.0 copy-start.2
  47.5 0.0 copy-start.3
  47.5 0.0 copy-start.5
  47.5 2.2 %reshape.35.x_ref = bf16[64,4096]{1,0:T(8,128)(2,1)S(1)} reshape(bf16[64,64,64]{2,1,0:T(8,128)(2,1)} %multiply_convert_fusion) | data formatting | bytes 1048576 | tf_op jit(solution)/shard_map/reshape | solution.py:412
  49.7 12.2 %regroup_rows.1.refs_0_ = bf16[256,1536]{1,0:T(8,128)(2,1)S(1)} custom-call(bf16[64,4096]{1,0:T(8,128)(2,1)S(1)} %reshape.35.x_ref), custom_call_target="tpu_custom_call" | custom-call | tf_op jit(solution)/shard_map/regroup_rows/pallas_call | solution.py:109
  61.9 0.0 copy-done.1
  61.9 0.0 copy-done.2
  61.9 0.0 copy-done.3
  61.9 0.0 copy-done.5
  61.9 67.3 %conv_backward.1 = (bf16[256,1024]{1,0:T(8,128)(2,1)S(1)}, f32[3,9,64,256]{3,2,1,0:T(8,128)S(1)}) custom-call(bf16[256,1536]{1,0:T(8,128)(2,1)S(1)} %regroup_rows.1.refs_0_, s32[3,256]{1,0:T(4,128)S(1)} %copy-done.5, bf16[3,9,256,256]{3,2,1,0:T(8,128)(2,1)} %refs_2_.1, bf16[256,1024]{1,0:T(8,128)(2,1)S(1)} %bitcast.26, bf16[256,1024]{1,0:T(8,128)(2,1)S(1)} %bitcast.27, ...), custom_call_target="tpu_custom_call" | custom-call | tf_op jit(solution)/shard_map/conv_backward/pallas_call | solution.py:339
  129.2 0.8 copy.26
  130.0 1.2 copy.27
  (4 shorter events, 0.1 us)
Async XLA Ops:
  0.6 1.2 copy-start
  3.6 2.3 %copy-start.7 = (s32[1,1024]{1,0:T(1,128)S(1)}, s32[1,1024]{1,0:T(1,128)}, u32[]{:S(2)}) copy-start(s32[1,1024]{1,0:T(1,128)} %param.14) | copy-start | bytes 12292
  3.6 2.3 %copy-start.4 = (bf16[1,64,4096]{2,1,0:T(8,128)(2,1)S(1)}, bf16[1,64,4096]{2,1,0:T(8,128)(2,1)}, u32[]{:S(2)}) copy-start(bf16[1,64,4096]{2,1,0:T(8,128)(2,1)} %param.10) | copy-start | bytes 1572868
  3.6 31.3 %copy-start.6 = (bf16[256,256]{1,0:T(8,128)(2,1)S(1)}, bf16[256,256]{1,0:T(8,128)(2,1)}, u32[]{:S(2)}) copy-start(bf16[256,256]{1,0:T(8,128)(2,1)} %param.11) | copy-start | bytes 393220
  47.5 14.4 %copy-start.1 = (bf16[1,256,1024]{2,1,0:T(8,128)(2,1)S(1)}, bf16[1,256,1024]{2,1,0:T(8,128)(2,1)}, u32[]{:S(2)}) copy-start(bf16[1,256,1024]{2,1,0:T(8,128)(2,1)} %param.15) | copy-start | bytes 1572868
  47.5 14.4 %copy-start.2 = (bf16[1,256,1024]{2,1,0:T(8,128)(2,1)S(1)}, bf16[1,256,1024]{2,1,0:T(8,128)(2,1)}, u32[]{:S(2)}) copy-start(bf16[1,256,1024]{2,1,0:T(8,128)(2,1)} %param.16) | copy-start | bytes 1572868
  47.5 14.4 %copy-start.3 = (bf16[1,256,1024]{2,1,0:T(8,128)(2,1)S(1)}, bf16[1,256,1024]{2,1,0:T(8,128)(2,1)}, u32[]{:S(2)}) copy-start(bf16[1,256,1024]{2,1,0:T(8,128)(2,1)} %param.17) | copy-start | bytes 1572868
  47.5 14.4 %copy-start.5 = (s32[3,256]{1,0:T(4,128)S(1)}, s32[3,256]{1,0:T(4,128)}, u32[]{:S(2)}) copy-start(s32[3,256]{1,0:T(4,128)} %refs_1_.1) | copy-start | bytes 9220

commit v4 on v3

--- a/solution.py
+++ b/solution.py
@@ -14,7 +14,7 @@
 HALO = MAXDIL * SIDE
 MESH = pl.DeviceIdType.MESH
 VMEM = pl.BlockSpec(memory_space=pltpu.VMEM)
-VMEM_LIMIT = 48 * 1024 * 1024
+VMEM_LIMIT = 34 * 1024 * 1024
 
 
 def enter(n):
@@ -28,51 +28,72 @@
     return me
 
 
-def gather_kernel(n, x_ref, g_ref, xo_ref, go_ref, x_send, x_recv, g_send, g_recv, own):
-    rows = x_ref.shape[0]
+def mix_kernel(n, x_ref, g_ref, w_ref, o_ref, go_ref, sites, mixed, *sems):
+    rows, cells = x_ref.shape
+    slab = cells // n
     me = enter(n)
-    place = pl.ds(pl.multiple_of(me * rows, rows), rows)
-    copies = []
-    for off in range(1, n):
-        peer = {"chan": lax.rem(me + off, n)}
-        copies.append(
-            pltpu.make_async_remote_copy(
-                src_ref=x_ref, dst_ref=xo_ref.at[place],
-                send_sem=x_send.at[off - 1], recv_sem=x_recv.at[off - 1],
-                device_id=peer, device_id_type=MESH,
+    own_rows = pl.ds(pl.multiple_of(me * rows, rows), rows)
+    own_cells = pl.ds(pl.multiple_of(me * slab, slab), slab)
+
+    def move(src, dst, place, off, to):
+        if off == 0:
+            copy = pltpu.make_async_copy(src, dst, sems[2 * place + 1].at[n - 1])
+        else:
+            copy = pltpu.make_async_remote_copy(
+                src_ref=src, dst_ref=dst,
+                send_sem=sems[2 * place].at[off - 1], recv_sem=sems[2 * place + 1].at[off - 1],
+                device_id={"chan": to}, device_id_type=MESH,
             )
+        copy.start()
+        return copy
+
+    turns = [(off, lax.rem(me + off, n)) for off in list(range(1, n)) + [0]]
+    copies = [
+        move(
+            x_ref.at[:, pl.ds(pl.multiple_of(to * slab, slab), slab)],
+            sites.at[own_rows], 0, off, to,
         )
-        copies.append(
-            pltpu.make_async_remote_copy(
-                src_ref=g_ref, dst_ref=go_ref.at[me],
-                send_sem=g_send.at[off - 1], recv_sem=g_recv.at[off - 1],
-                device_id=peer, device_id_type=MESH,
-            )
-        )
-    copies.append(pltpu.make_async_copy(x_ref, xo_ref.at[place], own.at[0]))
-    copies.append(pltpu.make_async_copy(g_ref, go_ref.at[me], own.at[1]))
-    for copy in copies:
-        copy.start()
+        for off, to in turns
+    ]
+    gates = [move(g_ref, go_ref.at[me], 1, off, to) for off, to in turns]
     for copy in copies:
         copy.wait()
-
-
-def gather(n, x, gate):
+    for start in range(0, slab, 256):
+        part = jnp.dot(
+            w_ref[...], sites[:, start : start + 256], preferred_element_type=jnp.float32
+        )
+        mixed[:, start : start + 256] = part.astype(jnp.bfloat16)
+    copies = [
+        move(
+            mixed.at[pl.ds(pl.multiple_of(to * rows, rows), rows)],
+            o_ref.at[:, own_cells], 2, off, to,
+        )
+        for off, to in turns
+    ]
+    for copy in gates + copies:
+        copy.wait()
+
+
+def mix(n, x, gate, weight):
     rows, cells = x.shape
     return pl.pallas_call(
-        functools.partial(gather_kernel, n),
+        functools.partial(mix_kernel, n),
         out_shape=(
-            jax.ShapeDtypeStruct((n * rows, cells), x.dtype),
+            jax.ShapeDtypeStruct((rows, cells), jnp.bfloat16),
             jax.ShapeDtypeStruct((n,) + gate.shape, gate.dtype),
         ),
-        in_specs=[VMEM, VMEM],
+        in_specs=[VMEM] * 3,
         out_specs=(VMEM, VMEM),
-        scratch_shapes=[pltpu.SemaphoreType.DMA((n - 1,))] * 4 + [pltpu.SemaphoreType.DMA((2,))],
+        scratch_shapes=[
+            pltpu.VMEM((n * rows, cells // n), jnp.bfloat16),
+            pltpu.VMEM((n * rows, cells // n), jnp.bfloat16),
+        ]
+        + [pltpu.SemaphoreType.DMA((n,))] * 6,
         compiler_params=pltpu.CompilerParams(
-            collective_id=0, has_side_effects=True, vmem_limit_bytes=VMEM_LIMIT
+            collective_id=0, has_side_effects=True, vmem_limit_bytes=12 * 1024 * 1024
         ),
-        name="gather_blocks",
-    )(x, gate)
+        name="mix_channels",
+    )(x, gate, weight)
 
 
 def regroup_kernel(n, x_ref, o_ref, send, recv, own):
@@ -113,7 +134,7 @@
         out_specs=VMEM,
         scratch_shapes=[pltpu.SemaphoreType.DMA((n - 1, 3))] * 2 + [pltpu.SemaphoreType.DMA((3,))],
         compiler_params=pltpu.CompilerParams(
-            collective_id=1, has_side_effects=True, vmem_limit_bytes=VMEM_LIMIT
+            collective_id=1, has_side_effects=True, vmem_limit_bytes=8 * 1024 * 1024
         ),
         name="regroup_rows",
     )(x)
@@ -387,15 +408,10 @@
     side = corr_kernels.shape[3]
     n = lax.axis_size("chan")
     slab = layer_input.shape[2]
-    own_start = lax.axis_index("chan") * chan_block
     gate = jnp.where(spin_up == 1, 1.5, 0.5).astype(jnp.float32)
     gate = jnp.broadcast_to(gate, (8, slab))
-    everything, gates = gather(n, out_cot[0], gate)
+    input_cot, gates = mix(n, out_cot[0], gate, mix_weight.T)
     gates = gates[:, 0, :].reshape(1, side, side)
-    own_columns = lax.dynamic_slice_in_dim(mix_weight, own_start, chan_block, 1)
-    input_cot = jnp.einsum(
-        "oc,on->cn", own_columns, everything, preferred_element_type=jnp.float32
-    )
     picked = lax.dynamic_index_in_dim(corr_kernels, momentum[0], axis=1, keepdims=False)
     positions = jnp.arange(side, dtype=jnp.int32)
     circ_table = (
@@ -404,7 +420,7 @@
     circulant = jnp.einsum(
         "aci,ixy->acxy", picked, circ_table, precision=lax.Precision.HIGHEST
     )
-    grid_values = input_cot.reshape(chan_block, side, side)
+    grid_values = input_cot.astype(jnp.float32).reshape(chan_block, side, side)
     high = lax.Precision.HIGH
     halfway = jnp.einsum("cxX,cxy->cXy", circulant[0], grid_values, precision=high)
     corr_grad = jnp.einsum("cXy,cyY->cXY", halfway, circulant[1], precision=high)

time: 131 us -> 121 us (0.924)
  Pallas kernels: 108 us -> 96.3 us
    pallas_call x1, Pallas kernels: 29 us -> 18.8 us  [mix(): pl.pallas_call(functools.partial(mix_kernel, n), out_shape=(jax.ShapeDtyp...]
    unnamed x18 -> x21, local copies, waits for them, and re-layouts: 2.43 us -> 4.53 us
    pallas_call x1, Pallas kernels: 67.3 us -> 65.5 us  [backward(): pl.pallas_call(functools.partial(backward_kernel, m, nz, norm), out_shape...]
where the time goes in v4:
time: 121 us; the launch traced here: 120 us
  Pallas kernels  96.3 us (80%)
  matrix products  12.2 us (10%)
  local copies, waits for them, and re-layouts  10.2 us (8%)
  between operations  1.53 us (1%)
    pallas_call x1, Pallas kernels, backward(): pl.pallas_call(functools.partial(backward_kernel, m, nz, norm), out_shape...  65.5 us
    pallas_call x1, Pallas kernels, mix(): pl.pallas_call(functools.partial(mix_kernel, n), out_shape=(jax.ShapeDtyp...  18.8 us
    pallas_call x1, Pallas kernels, regroup(): pl.pallas_call(functools.partial(regroup_kernel, n), out_shape=jax.ShapeD...  12 us
    dot_general x1, matrix products, on_device(): jnp.einsum('cXy,cyY->cXY', halfway, circulant[1], precision=high)  5.45 us
    dot_general x1, matrix products, on_device(): jnp.einsum('cxX,cxy->cXy', circulant[0], grid_values, precision=high)  4.97 us
    unnamed x21, local copies, waits for them, and re-layouts  4.53 us

profile of v4, /device:TPU:0, one launch (start us, length us, event | category | flops | bytes accessed | tf_op | source)
XLA Modules:
  0.0 120.3 jit_solution(8129175141550002531)
XLA Ops:
  0.6 0.0 copy-start
  1.4 0.4 copy-done
  1.8 1.8 %fusion.5 = f32[2,64,64,64]{3,1,2,0:T(8,128)S(1)} fusion(s32[64,64]{1,0:T(8,128)S(1)} %add_select_fusion, f32[2,12,64,64]{3,2,1,0:T(8,128)S(1)} %copy-done, s32[]{:T(128)S(6)} %select_n.19), kind=kOutput, calls=%fused_computation.9 | convolution fusion | flops 402915328 | bytes 2195460 | tf_op jit(solution)/shard_map/aci,ixy->acxy/dot_general | solution.py:420
  3.6 0.0 copy-start.7
  3.6 0.0 copy-start.8
  3.6 0.0 copy-start.5
  3.6 2.3 %slice_bitcast_fusion = (f32[64,64,64]{2,0,1:T(8,128)}, f32[64,64,64]{2,0,1:T(8,128)}) fusion(f32[2,64,64,64]{3,1,2,0:T(8,128)S(1)} %fusion.5), kind=kLoop, calls=%fused_computation | loop fusion | bytes 4194304 | tf_op jit(solution)/shard_map/squeeze | solution.py:426
  5.9 0.0 copy-done.7
  5.9 0.1 copy.12
  6.0 0.0 copy-done.8
  6.0 0.0 copy-done.5
  6.0 18.8 %mix_channels.1 = (bf16[64,4096]{1,0:T(8,128)(2,1)S(1)}, f32[4,8,1024]{2,1,0:T(8,128)S(1)}) custom-call(bf16[64,4096]{1,0:T(8,128)(2,1)S(1)} %bitcast.29, f32[8,1024]{1,0:T(8,128)S(1)} %broadcast_in_dim.25.g_ref, bf16[256,256]{1,0:T(8,128)(2,1)S(1)} %bitcast.31), custom_call_target="tpu_custom_call" | custom-call | tf_op jit(solution)/shard_map/mix_channels/pallas_call | solution.py:79
  24.9 1.1 reshape.34
  26.0 5.0 %fusion = f32[64,64,64]{2,1,0:T(8,128)} fusion(bf16[64,64,64]{2,1,0:T(8,128)(2,1)S(1)} %reshape.34, f32[64,64,64]{2,0,1:T(8,128)} %get-tuple-element.11), kind=kOutput, calls=%fused_computation.2 | convolution fusion | flops 100663296 | bytes 2621440 | tf_op jit(solution)/shard_map/cxX,cxy->cXy/dot_general | solution.py:425
  31.0 0.1 mul.10
  31.1 5.5 %multiply_convert_fusion = bf16[64,64,64]{2,1,0:T(8,128)(2,1)} fusion(f32[64,64,64]{2,1,0:T(8,128)} %fusion, f32[64,64,64]{2,0,1:T(8,128)} %get-tuple-element.10, f32[64,64]{1,0:T(8,128)S(1)} %mul.10), kind=kOutput, calls=%fused_computation.6 | convolution fusion | flops 101711872 | bytes 2637824 | tf_op jit(solution)/shard_map/cXy,cyY->cXY/dot_general | solution.py:426
  36.6 0.0 copy-start.2
  36.6 0.0 copy-start.3
  36.6 0.0 copy-start.4
  36.6 0.0 copy-start.6
  36.6 2.2 %reshape.35.x_ref = bf16[64,4096]{1,0:T(8,128)(2,1)S(1)} reshape(bf16[64,64,64]{2,1,0:T(8,128)(2,1)} %multiply_convert_fusion) | data formatting | bytes 1048576 | tf_op jit(solution)/shard_map/reshape | solution.py:428
  38.8 12.0 %regroup_rows.1.refs_0_ = bf16[256,1536]{1,0:T(8,128)(2,1)S(1)} custom-call(bf16[64,4096]{1,0:T(8,128)(2,1)S(1)} %reshape.35.x_ref), custom_call_target="tpu_custom_call" | custom-call | tf_op jit(solution)/shard_map/regroup_rows/pallas_call | solution.py:130
  50.8 0.0 copy-done.2
  50.8 0.0 copy-done.3
  50.8 0.0 copy-done.4
  50.8 0.0 copy-done.6
  50.8 0.0 copy-start.1
  50.8 2.0 %copy-done.1 = bf16[3,9,256,256]{3,2,1,0:T(8,128)(2,1)S(1)} copy-done((bf16[3,9,256,256]{3,2,1,0:T(8,128)(2,1)S(1)}, bf16[3,9,256,256]{3,2,1,0:T(8,128)(2,1)}, u32[]{:S(2)}) %copy-start.1) | copy-done | bytes 3538968
  52.8 65.5 %conv_backward.1 = (bf16[256,1024]{1,0:T(8,128)(2,1)S(1)}, f32[3,9,64,256]{3,2,1,0:T(8,128)S(1)}) custom-call(bf16[256,1536]{1,0:T(8,128)(2,1)S(1)} %regroup_rows.1.refs_0_, s32[3,256]{1,0:T(4,128)S(1)} %copy-done.6, bf16[3,9,256,256]{3,2,1,0:T(8,128)(2,1)S(1)} %copy-done.1, bf16[256,1024]{1,0:T(8,128)(2,1)S(1)} %bitcast.26, bf16[256,1024]{1,0:T(8,128)(2,1)S(1)} %bitcast.27, ...), custom_call_target="tpu_custom_call" | custom-call | tf_op jit(solution)/shard_map/conv_backward/pallas_call | solution.py:360
  118.3 0.8 copy.27
  119.1 1.2 %copy.28 = f32[3,9,64,256]{3,2,1,0:T(8,128)} copy(f32[3,9,64,256]{3,2,1,0:T(8,128)S(1)} %get-tuple-element.15) | data formatting | bytes 3538944
  (4 shorter events, 0.1 us)
Async XLA Ops:
  0.6 1.2 copy-start
  3.6 2.3 %copy-start.7 = (bf16[256,256]{1,0:T(8,128)(2,1)S(1)}, bf16[256,256]{1,0:T(8,128)(2,1)}, u32[]{:S(2)}) copy-start(bf16[256,256]{1,0:T(8,128)(2,1)} %param.11) | copy-start | bytes 393220
  3.6 2.4 %copy-start.8 = (s32[1,1024]{1,0:T(1,128)S(1)}, s32[1,1024]{1,0:T(1,128)}, u32[]{:S(2)}) copy-start(s32[1,1024]{1,0:T(1,128)} %param.14) | copy-start | bytes 12292
  3.6 2.4 %copy-start.5 = (bf16[1,64,4096]{2,1,0:T(8,128)(2,1)S(1)}, bf16[1,64,4096]{2,1,0:T(8,128)(2,1)}, u32[]{:S(2)}) copy-start(bf16[1,64,4096]{2,1,0:T(8,128)(2,1)} %param.10) | copy-start | bytes 1572868
  36.6 14.2 %copy-start.2 = (bf16[1,256,1024]{2,1,0:T(8,128)(2,1)S(1)}, bf16[1,256,1024]{2,1,0:T(8,128)(2,1)}, u32[]{:S(2)}) copy-start(bf16[1,256,1024]{2,1,0:T(8,128)(2,1)} %param.15) | copy-start | bytes 1572868
  36.6 14.2 %copy-start.3 = (bf16[1,256,1024]{2,1,0:T(8,128)(2,1)S(1)}, bf16[1,256,1024]{2,1,0:T(8,128)(2,1)}, u32[]{:S(2)}) copy-start(bf16[1,256,1024]{2,1,0:T(8,128)(2,1)} %param.16) | copy-start | bytes 1572868
  36.6 14.2 %copy-start.4 = (bf16[1,256,1024]{2,1,0:T(8,128)(2,1)S(1)}, bf16[1,256,1024]{2,1,0:T(8,128)(2,1)}, u32[]{:S(2)}) copy-start(bf16[1,256,1024]{2,1,0:T(8,128)(2,1)} %param.17) | copy-start | bytes 1572868
  36.6 14.2 %copy-start.6 = (s32[3,256]{1,0:T(4,128)S(1)}, s32[3,256]{1,0:T(4,128)}, u32[]{:S(2)}) copy-start(s32[3,256]{1,0:T(4,128)} %refs_1_.1) | copy-start | bytes 9220
  50.8 2.0 %copy-start.1 = (bf16[3,9,256,256]{3,2,1,0:T(8,128)(2,1)S(1)}, bf16[3,9,256,256]{3,2,1,0:T(8,128)(2,1)}, u32[]{:S(2)}) copy-start(bf16[3,9,256,256]{3,2,1,0:T(8,128)(2,1)} %refs_2_.1) | copy-start | bytes 10616836

commit v5 on v4

--- a/solution.py
+++ b/solution.py
@@ -283,8 +283,8 @@
             return carry
 
         lax.fori_loop(0, side_rows + 2 * MAXDIL, shift_columns, 0)
-        if level < LAYERS - 1:
-            pair_to_chan(level + 1)
+        if level == 0:
+            pair_to_chan(1)
         picks = [(step == d).astype(f32).astype(bf16) for d in range(1, MAXDIL + 1)]
 
         def shift_rows(r, carry, picks=picks):
@@ -326,6 +326,8 @@
                     sems[10:12], (level - 1, 1), down,
                 ),
             ]
+            if level < LAYERS - 1:
+                pair_to_chan(level + 1)
             act = jnp.tanh(saved[level][...].astype(f32)).astype(bf16)
         else:
             chan_to_z(LAYERS - 1)

time: 121 us -> 120 us (level)
  no operation moved by 1% of the time
where the time goes in v5:
time: 120 us
  Pallas kernels  95.9 us (80%)
  matrix products  12.2 us (10%)
  local copies, waits for them, and re-layouts  10.2 us (8%)
  between operations  1.53 us (1%)
    pallas_call x1, Pallas kernels, backward(): pl.pallas_call(functools.partial(backward_kernel, m, nz, norm), out_shape...  65 us
    pallas_call x1, Pallas kernels, mix(): pl.pallas_call(functools.partial(mix_kernel, n), out_shape=(jax.ShapeDtyp...  18.8 us
    pallas_call x1, Pallas kernels, regroup(): pl.pallas_call(functools.partial(regroup_kernel, n), out_shape=jax.ShapeD...  12 us
    dot_general x1, matrix products, on_device(): jnp.einsum('cXy,cyY->cXY', halfway, circulant[1], precision=high)  5.45 us
    dot_general x1, matrix products, on_device(): jnp.einsum('cxX,cxy->cXy', circulant[0], grid_values, precision=high)  4.97 us
    unnamed x21, local copies, waits for them, and re-layouts  4.53 us

profile of v5, /device:TPU:0, one launch (start us, length us, event | category | flops | bytes accessed | tf_op | source)
XLA Modules:
  0.0 119.9 jit_solution(11701614348984530980)
XLA Ops:
  0.6 0.0 copy-start
  1.4 0.4 copy-done
  1.8 1.8 %fusion.5 = f32[2,64,64,64]{3,1,2,0:T(8,128)S(1)} fusion(s32[64,64]{1,0:T(8,128)S(1)} %add_select_fusion, f32[2,12,64,64]{3,2,1,0:T(8,128)S(1)} %copy-done, s32[]{:T(128)S(6)} %select_n.19), kind=kOutput, calls=%fused_computation.9 | convolution fusion | flops 402915328 | bytes 2195460 | tf_op jit(solution)/shard_map/aci,ixy->acxy/dot_general | solution.py:422
  3.6 0.0 copy-start.7
  3.6 0.0 copy-start.8
  3.6 0.0 copy-start.5
  3.6 2.3 %slice_bitcast_fusion = (f32[64,64,64]{2,0,1:T(8,128)}, f32[64,64,64]{2,0,1:T(8,128)}) fusion(f32[2,64,64,64]{3,1,2,0:T(8,128)S(1)} %fusion.5), kind=kLoop, calls=%fused_computation | loop fusion | bytes 4194304 | tf_op jit(solution)/shard_map/squeeze | solution.py:428
  5.9 0.0 copy-done.7
  5.9 0.1 copy.12
  6.0 0.0 copy-done.8
  6.0 0.0 copy-done.5
  6.0 18.8 %mix_channels.1 = (bf16[64,4096]{1,0:T(8,128)(2,1)S(1)}, f32[4,8,1024]{2,1,0:T(8,128)S(1)}) custom-call(bf16[64,4096]{1,0:T(8,128)(2,1)S(1)} %bitcast.29, f32[8,1024]{1,0:T(8,128)S(1)} %broadcast_in_dim.25.g_ref, bf16[256,256]{1,0:T(8,128)(2,1)S(1)} %bitcast.31), custom_call_target="tpu_custom_call" | custom-call | tf_op jit(solution)/shard_map/mix_channels/pallas_call | solution.py:79
  24.9 1.1 reshape.34
  26.0 5.0 %fusion = f32[64,64,64]{2,1,0:T(8,128)} fusion(bf16[64,64,64]{2,1,0:T(8,128)(2,1)S(1)} %reshape.34, f32[64,64,64]{2,0,1:T(8,128)} %get-tuple-element.11), kind=kOutput, calls=%fused_computation.2 | convolution fusion | flops 100663296 | bytes 2621440 | tf_op jit(solution)/shard_map/cxX,cxy->cXy/dot_general | solution.py:427
  31.0 0.1 mul.10
  31.1 5.5 %multiply_convert_fusion = bf16[64,64,64]{2,1,0:T(8,128)(2,1)} fusion(f32[64,64,64]{2,1,0:T(8,128)} %fusion, f32[64,64,64]{2,0,1:T(8,128)} %get-tuple-element.10, f32[64,64]{1,0:T(8,128)S(1)} %mul.10), kind=kOutput, calls=%fused_computation.6 | convolution fusion | flops 101711872 | bytes 2637824 | tf_op jit(solution)/shard_map/cXy,cyY->cXY/dot_general | solution.py:428
  36.6 0.0 copy-start.2
  36.6 0.0 copy-start.3
  36.6 0.0 copy-start.4
  36.6 0.0 copy-start.6
  36.6 2.2 %reshape.35.x_ref = bf16[64,4096]{1,0:T(8,128)(2,1)S(1)} reshape(bf16[64,64,64]{2,1,0:T(8,128)(2,1)} %multiply_convert_fusion) | data formatting | bytes 1048576 | tf_op jit(solution)/shard_map/reshape | solution.py:430
  38.8 12.0 %regroup_rows.1.refs_0_ = bf16[256,1536]{1,0:T(8,128)(2,1)S(1)} custom-call(bf16[64,4096]{1,0:T(8,128)(2,1)S(1)} %reshape.35.x_ref), custom_call_target="tpu_custom_call" | custom-call | tf_op jit(solution)/shard_map/regroup_rows/pallas_call | solution.py:130
  50.8 0.0 copy-done.2
  50.8 0.0 copy-done.3
  50.8 0.0 copy-done.4
  50.8 0.0 copy-done.6
  50.8 0.0 copy-start.1
  50.8 2.0 %copy-done.1 = bf16[3,9,256,256]{3,2,1,0:T(8,128)(2,1)S(1)} copy-done((bf16[3,9,256,256]{3,2,1,0:T(8,128)(2,1)S(1)}, bf16[3,9,256,256]{3,2,1,0:T(8,128)(2,1)}, u32[]{:S(2)}) %copy-start.1) | copy-done | bytes 3538968
  52.8 65.0 %conv_backward.1 = (bf16[256,1024]{1,0:T(8,128)(2,1)S(1)}, f32[3,9,64,256]{3,2,1,0:T(8,128)S(1)}) custom-call(bf16[256,1536]{1,0:T(8,128)(2,1)S(1)} %regroup_rows.1.refs_0_, s32[3,256]{1,0:T(4,128)S(1)} %copy-done.6, bf16[3,9,256,256]{3,2,1,0:T(8,128)(2,1)S(1)} %copy-done.1, bf16[256,1024]{1,0:T(8,128)(2,1)S(1)} %bitcast.26, bf16[256,1024]{1,0:T(8,128)(2,1)S(1)} %bitcast.27, ...), custom_call_target="tpu_custom_call" | custom-call | tf_op jit(solution)/shard_map/conv_backward/pallas_call | solution.py:362
  117.9 0.8 copy.27
  118.6 1.2 %copy.28 = f32[3,9,64,256]{3,2,1,0:T(8,128)} copy(f32[3,9,64,256]{3,2,1,0:T(8,128)S(1)} %get-tuple-element.15) | data formatting | bytes 3538944
  (4 shorter events, 0.1 us)
Async XLA Ops:
  0.6 1.2 copy-start
  3.6 2.3 %copy-start.7 = (bf16[256,256]{1,0:T(8,128)(2,1)S(1)}, bf16[256,256]{1,0:T(8,128)(2,1)}, u32[]{:S(2)}) copy-start(bf16[256,256]{1,0:T(8,128)(2,1)} %param.11) | copy-start | bytes 393220
  3.6 2.4 %copy-start.8 = (s32[1,1024]{1,0:T(1,128)S(1)}, s32[1,1024]{1,0:T(1,128)}, u32[]{:S(2)}) copy-start(s32[1,1024]{1,0:T(1,128)} %param.14) | copy-start | bytes 12292
  3.6 2.4 %copy-start.5 = (bf16[1,64,4096]{2,1,0:T(8,128)(2,1)S(1)}, bf16[1,64,4096]{2,1,0:T(8,128)(2,1)}, u32[]{:S(2)}) copy-start(bf16[1,64,4096]{2,1,0:T(8,128)(2,1)} %param.10) | copy-start | bytes 1572868
  36.6 14.2 %copy-start.2 = (bf16[1,256,1024]{2,1,0:T(8,128)(2,1)S(1)}, bf16[1,256,1024]{2,1,0:T(8,128)(2,1)}, u32[]{:S(2)}) copy-start(bf16[1,256,1024]{2,1,0:T(8,128)(2,1)} %param.15) | copy-start | bytes 1572868
  36.6 14.2 %copy-start.3 = (bf16[1,256,1024]{2,1,0:T(8,128)(2,1)S(1)}, bf16[1,256,1024]{2,1,0:T(8,128)(2,1)}, u32[]{:S(2)}) copy-start(bf16[1,256,1024]{2,1,0:T(8,128)(2,1)} %param.16) | copy-start | bytes 1572868
  36.6 14.2 %copy-start.4 = (bf16[1,256,1024]{2,1,0:T(8,128)(2,1)S(1)}, bf16[1,256,1024]{2,1,0:T(8,128)(2,1)}, u32[]{:S(2)}) copy-start(bf16[1,256,1024]{2,1,0:T(8,128)(2,1)} %param.17) | copy-start | bytes 1572868
  36.6 14.2 %copy-start.6 = (s32[3,256]{1,0:T(4,128)S(1)}, s32[3,256]{1,0:T(4,128)}, u32[]{:S(2)}) copy-start(s32[3,256]{1,0:T(4,128)} %refs_1_.1) | copy-start | bytes 9220
  50.8 2.0 %copy-start.1 = (bf16[3,9,256,256]{3,2,1,0:T(8,128)(2,1)S(1)}, bf16[3,9,256,256]{3,2,1,0:T(8,128)(2,1)}, u32[]{:S(2)}) copy-start(bf16[3,9,256,256]{3,2,1,0:T(8,128)(2,1)} %refs_2_.1) | copy-start | bytes 10616836
